TPU v7x, 512 devices: a whole 4x8x8 slice. The times are simulated.
512 devices in a mesh: group: 16 (over x, z_hi), shard: 32 (over y, z_lo, core).
Axes of the slice: x: 4, y: 8, z: 8 (z_hi: 4, z_lo: 2; z = z_hi * 2 + z_lo), core: 2. Of those that a mesh axis runs over, the one named last changes fastest.
Arguments:
- tokens: bfloat16 [32768, 2048], P(('group', 'shard')), may hold values from -7 to 7
- w_qk: bfloat16 [2048, 1024], P('shard'), may hold values from -0.09375 to 0.09375
- w_in: bfloat16 [128, 2048], replicated, may hold values from -0.5 to 0.5
- w_out: bfloat16 [2048, 128], replicated, may hold values from -0.125 to 0.125
- particles: bfloat16 [2097152, 128], P(('group', 'shard')), may hold values from -6 to 6
- cotangent: bfloat16 [2097152, 128], P(('group', 'shard')), may hold values from -6 to 6
- clusters: int32 [2097152], P(('group', 'shard')), may hold values from 0 to 63
- owners: int32 [16384], P(('group', 'shard')), may hold values from 0 to 31, as said below
Outputs:
- particle_out: bfloat16 [2097152, 128], P(('group', 'shard'))
- qk_grad: float32 [2048, 1024], P('shard')
Inputs may be any that keep to these rules, and one draw needn't show every extreme that they name: `owners`: each device's blocks name one owner at most 2 times; in every group some owner is named exactly 2 times by the blocks of every device of the group.
All inputs are finite; a program needn't handle non-finite values.
Results may differ from a plain program's by a relative error of at most 0.028.
Values may be sent and summed in bfloat16 or wider, within the bound.
A program may use at most 64 MiB of HBM per device.

v0:
```python
import math

import jax
import jax.numpy as jnp
from jax import lax
from jax.sharding import PartitionSpec as P

HEADS = 8


def token_pass(tokens, pooled, w_qk, w_in, w_out, pooled_grad):
    hidden_sum = tokens.astype(jnp.float32) + jnp.dot(
        pooled, w_in, preferred_element_type=jnp.float32
    )
    hidden = hidden_sum.astype(jnp.bfloat16)
    queries = jnp.dot(hidden, w_qk, preferred_element_type=jnp.float32).astype(jnp.bfloat16)
    num_rows = hidden.shape[0]
    head_cols = queries.shape[1]
    q_heads = queries.reshape(num_rows, HEADS, -1).astype(jnp.float32)
    score_scale = 1.0 / math.sqrt(q_heads.shape[2])
    scores = jnp.einsum("ihd,jhd->hij", q_heads, q_heads) * score_scale
    self_mask = jnp.eye(num_rows, dtype=bool)
    scores = jnp.where(self_mask[None], -1000000000.0, scores)
    row_max = jnp.max(scores, axis=2, keepdims=True)
    weights_exp = jnp.exp(scores - row_max)
    attn_prob = weights_exp / jnp.sum(weights_exp, axis=2, keepdims=True)
    prob_low = lax.optimization_barrier(attn_prob.astype(jnp.bfloat16)).astype(jnp.float32)
    hidden_wide = hidden.astype(jnp.float32)
    values = hidden_wide[:, :head_cols].reshape(num_rows, HEADS, -1)
    attended = jnp.einsum("hij,jhv->ihv", prob_low, values).reshape(num_rows, head_cols)
    output = jnp.concatenate(
        [hidden_wide[:, :head_cols] + attended, hidden_wide[:, head_cols:]], axis=1
    ).astype(jnp.bfloat16)
    unpooled = jnp.dot(output, w_out, preferred_element_type=jnp.float32).astype(jnp.bfloat16)
    out_grad = jnp.dot(pooled_grad, w_out.T, preferred_element_type=jnp.float32).astype(
        jnp.bfloat16
    )
    grad_heads = out_grad[:, :head_cols].reshape(num_rows, HEADS, -1).astype(jnp.float32)
    prob_grad = jnp.einsum("ihv,jhv->hij", grad_heads, values)
    score_grad = (
        attn_prob
        * (prob_grad - jnp.sum(prob_grad * attn_prob, axis=2, keepdims=True))
        * score_scale
    )
    score_low = lax.optimization_barrier(score_grad.astype(jnp.bfloat16)).astype(jnp.float32)
    q_grad = jnp.einsum("hij,jhd->ihd", score_low, q_heads) + jnp.einsum(
        "hji,jhd->ihd", score_low, q_heads
    )
    q_grad = q_grad.reshape(num_rows, -1).astype(jnp.bfloat16)
    return (unpooled, hidden, q_grad)


def local(tokens, w_qk, w_in, w_out, particles, cotangent, clusters, owners):
    n_shard = lax.axis_size("shard")
    num_blocks = owners.shape[0]
    block_rows = particles.shape[0] // num_blocks
    channels = particles.shape[1]
    capacity = 2 * num_blocks // n_shard
    slot_count = n_shard * capacity
    t_rows = tokens.shape[0]
    owner_hot = (owners[:, None] == jnp.arange(n_shard, dtype=jnp.int32)[None, :]).astype(jnp.int32)
    earlier = jnp.cumsum(owner_hot, axis=0) - owner_hot
    slot_rank = jnp.sum(earlier * owner_hot, axis=1)
    target = owners * capacity + slot_rank
    placing = (target[None, :] == jnp.arange(slot_count, dtype=jnp.int32)[:, None]).astype(
        jnp.bfloat16
    )
    feat_rows = particles.reshape(num_blocks, block_rows * channels)
    grad_rows = cotangent.reshape(num_blocks, block_rows * channels)
    send_feat = jnp.dot(placing, feat_rows, preferred_element_type=jnp.float32).astype(jnp.bfloat16)
    send_grad = jnp.dot(placing, grad_rows, preferred_element_type=jnp.float32).astype(jnp.bfloat16)
    label_rows = (clusters.reshape(num_blocks, block_rows) + 1).astype(jnp.float32)
    send_label = (
        jnp.dot(placing.astype(jnp.float32), label_rows, precision=lax.Precision.HIGHEST) - 1.0
    )
    send_feat = send_feat.reshape(n_shard, capacity, block_rows, channels)
    send_grad = send_grad.reshape(n_shard, capacity, block_rows, channels)
    send_label = send_label.astype(jnp.bfloat16).reshape(n_shard, capacity, block_rows)
    got_feat, got_grad, got_label = (
        lax.all_to_all(send_feat, "shard", split_axis=0, concat_axis=0, tiled=True),
        lax.all_to_all(send_grad, "shard", split_axis=0, concat_axis=0, tiled=True),
        lax.all_to_all(send_label, "shard", split_axis=0, concat_axis=0, tiled=True),
    )
    received = slot_count * block_rows
    labels = got_label.reshape(received).astype(jnp.float32)
    member = (labels[None, :] == jnp.arange(t_rows, dtype=jnp.float32)[:, None]).astype(
        jnp.bfloat16
    )
    counts = jnp.sum(member, axis=1, dtype=jnp.float32)
    pooled_sum = jnp.dot(
        member, got_feat.reshape(received, channels), preferred_element_type=jnp.float32
    )
    pooled = (pooled_sum / jnp.maximum(counts, 1.0)[:, None]).astype(jnp.bfloat16)
    pooled_grad = jnp.dot(
        member, got_grad.reshape(received, channels), preferred_element_type=jnp.float32
    ).astype(jnp.bfloat16)
    full_qk = lax.all_gather(w_qk, "shard", axis=0, tiled=True)
    unpooled, hidden, q_grad = token_pass(tokens, pooled, full_qk, w_in, w_out, pooled_grad)
    slot_values = jnp.einsum(
        "ts,tw->sw", member, unpooled, preferred_element_type=jnp.float32
    ).astype(jnp.bfloat16)
    slot_values = slot_values.reshape(n_shard, capacity, block_rows, channels)
    returned = lax.all_to_all(slot_values, "shard", split_axis=0, concat_axis=0, tiled=True)
    returned_rows = jnp.einsum(
        "sb,sx->bx",
        placing,
        returned.reshape(slot_count, block_rows * channels),
        preferred_element_type=jnp.float32,
    )
    returned_rows = returned_rows.reshape(num_blocks * block_rows, channels)
    particle_out = (particles.astype(jnp.float32) + returned_rows).astype(jnp.bfloat16)
    shard_sum = lax.psum_scatter(
        jnp.einsum("td,tk->dk", hidden, q_grad, preferred_element_type=jnp.float32).astype(
            jnp.bfloat16
        ),
        "shard",
        scatter_dimension=0,
        tiled=True,
    )
    qk_grad = lax.psum(shard_sum, "group").astype(jnp.float32)
    return (particle_out, qk_grad)


def solution(mesh):
    placed = (
        P(("group", "shard"), None),
        P("shard", None),
        P(),
        P(),
        P(("group", "shard"), None),
        P(("group", "shard"), None),
        P(("group", "shard")),
        P(("group", "shard")),
    )
    return jax.shard_map(
        local,
        mesh=mesh,
        in_specs=placed,
        out_specs=(P(("group", "shard"), None), P("shard", None)),
        check_vma=False,
    )
```

profile of v0, /device:TPU:16, one launch (start us, length us, event | category | flops | bytes accessed | tf_op | source)
XLA Modules:
  0.0 490.9 jit_solution(13615514162843825497)
XLA Ops:
  9.5 1.5 fusion.22
  11.0 9.4 %all-to-all-start = ((bf16[32,2,128]{2,1,0:T(2,128)(2,1)}), bf16[32,2,128]{2,1,0:T(2,128)(2,1)S(1)}, u32[]{:S(2)}, u32[]{:S(2)}) async-start(bf16[32,2,128]{2,1,0:T(2,128)(2,1)} %bitcast.1), calls=%async_computation | async-start | bytes 32768 | tf_op jit(solution)/shard_map/all_to_all | solution.py:82
  20.4 1.5 reshape.76
  22.6 1.9 copy.49
  24.5 2.0 all-to-all-done
  26.6 6.2 %all-to-all-start.1 = ((bf16[32,2,128,128]{3,2,1,0:T(8,128)(2,1)}), bf16[32,2,128,128]{3,2,1,0:T(8,128)(2,1)S(1)}, u32[]{:S(2)}, u32[]{:S(2)}) async-start(bf16[32,2,128,128]{3,2,1,0:T(8,128)(2,1)} %bitcast.79), calls=%async_computation.1 | async-start | bytes 4194304 | tf_op jit(solution)/shard_map/all_to_all | solution.py:80
  33.5 2.3 reshape.85
  35.8 1.9 fusion.10
  37.8 1.9 copy.51
  39.7 51.1 %all-to-all-done.1 = bf16[32,2,128,128]{3,2,1,0:T(8,128)(2,1)S(1)} async-done(((bf16[32,2,128,128]{3,2,1,0:T(8,128)(2,1)}), bf16[32,2,128,128]{3,2,1,0:T(8,128)(2,1)S(1)}, u32[]{:S(2)}, u32[]{:S(2)}) %all-to-all-start.1) | async-done | bytes 2097184 | tf_op jit(solution)/shard_map/all_to_all | solution.py:80
  90.8 8.4 %all-to-all-start.3 = ((bf16[32,2,128,128]{3,2,1,0:T(8,128)(2,1)}), bf16[32,2,128,128]{3,2,1,0:T(8,128)(2,1)}, u32[]{:S(2)}, u32[]{:S(2)}) async-start(bf16[32,2,128,128]{3,2,1,0:T(8,128)(2,1)} %bitcast.78), calls=%async_computation.3 | async-start | bytes 4194304 | tf_op jit(solution)/shard_map/all_to_all | solution.py:81
  99.6 1.6 fusion.2
  101.2 53.0 %all-to-all-done.3 = bf16[32,2,128,128]{3,2,1,0:T(8,128)(2,1)} async-done(((bf16[32,2,128,128]{3,2,1,0:T(8,128)(2,1)}), bf16[32,2,128,128]{3,2,1,0:T(8,128)(2,1)}, u32[]{:S(2)}, u32[]{:S(2)}) %all-to-all-start.3) | async-done | bytes 2097184 | tf_op jit(solution)/shard_map/all_to_all | solution.py:81
  154.2 2.3 fusion.25
  156.7 3.0 fusion.19
  160.5 3.2 convolution_convert_fusion.3
  164.1 1.3 convolution_convert_fusion.2
  165.4 58.8 %all_to_all.20 = bf16[32,2,128,128]{3,2,1,0:T(8,128)(2,1)S(1)} all-to-all(bf16[32,2,128,128]{3,2,1,0:T(8,128)(2,1)S(1)} %bitcast.80), channel_id=1, replica_groups=mesh['group'=16,'shard'=32] {'shard'}, dimensions={0} | all-to-all | bytes 4194304 | tf_op jit(solution)/shard_map/all_to_all | solution.py:103
  224.2 2.8 fusion.3
  227.0 1.7 reshape.84
  228.7 63.8 %reduce-scatter.2.cloned.1.call-done = bf16[64,1024]{1,0:T(8,128)(2,1)} async-done(((bf16[2048,1024]{1,0:T(8,128)(2,1)}), bf16[64,1024]{1,0:T(8,128)(2,1)}) %reduce-scatter.2.cloned.1.call-update) | async-done | bytes 131088 | tf_op jit(solution)/shard_map/reduce_scatter | solution.py:112
  292.5 2.4 add_convert_fusion
  294.9 187.8 %all-reduce.2.cloned.1.call-done = bf16[64,1024]{1,0:T(8,128)(2,1)} async-done(((bf16[64,1024]{1,0:T(8,128)(2,1)}), bf16[64,1024]{1,0:T(8,128)(2,1)}) %all-reduce.2.cloned.1.call-update) | async-done | bytes 131088 | tf_op jit(solution)/shard_map/psum | solution.py:120
  482.8 1.6 convert_element_type.119
  (29 shorter events, 5.5 us)
Async XLA Ops:
  7.2 147.0 %copy-start = (bf16[2048,128]{1,0:T(8,128)(2,1)S(1)}, bf16[2048,128]{1,0:T(8,128)(2,1)}, u32[]{:S(2)}) copy-start(bf16[2048,128]{1,0:T(8,128)(2,1)} %param.11) | copy-start | bytes 1572868
  11.0 15.6 %all-to-all-start = ((bf16[32,2,128]{2,1,0:T(2,128)(2,1)}), bf16[32,2,128]{2,1,0:T(2,128)(2,1)S(1)}, u32[]{:S(2)}, u32[]{:S(2)}) async-start(bf16[32,2,128]{2,1,0:T(2,128)(2,1)} %bitcast.1), calls=%async_computation | async-start | bytes 32768 | tf_op jit(solution)/shard_map/all_to_all | solution.py:82
  26.6 64.2 %all-to-all-start.1 = ((bf16[32,2,128,128]{3,2,1,0:T(8,128)(2,1)}), bf16[32,2,128,128]{3,2,1,0:T(8,128)(2,1)S(1)}, u32[]{:S(2)}, u32[]{:S(2)}) async-start(bf16[32,2,128,128]{3,2,1,0:T(8,128)(2,1)} %bitcast.79), calls=%async_computation.1 | async-start | bytes 4194304 | tf_op jit(solution)/shard_map/all_to_all | solution.py:80
  32.8 123.9 %all-gather.2.cloned.1.call-start = ((), (), s32[]{:S(2)}) async-start(), calls=%async_computation.5 | async-start | bytes 4325376 | tf_op jit(solution)/shard_map/all_gather | solution.py:97
  90.8 8.8 %copy-start.1 = (bf16[128,2048]{1,0:T(8,128)(2,1)S(1)}, bf16[128,2048]{1,0:T(8,128)(2,1)}, u32[]{:S(2)}) copy-start(bf16[128,2048]{1,0:T(8,128)(2,1)} %param.10) | copy-start | bytes 1572868
  90.8 63.4 %all-to-all-start.3 = ((bf16[32,2,128,128]{3,2,1,0:T(8,128)(2,1)}), bf16[32,2,128,128]{3,2,1,0:T(8,128)(2,1)}, u32[]{:S(2)}, u32[]{:S(2)}) async-start(bf16[32,2,128,128]{3,2,1,0:T(8,128)(2,1)} %bitcast.78), calls=%async_computation.3 | async-start | bytes 4194304 | tf_op jit(solution)/shard_map/all_to_all | solution.py:81
  99.2 193.3 %reduce-scatter.2.cloned.1.call-start = ((), (), s32[]{:S(2)}) async-start(), calls=%async_computation.6 | async-start | bytes 4325376 | tf_op jit(solution)/shard_map/reduce_scatter | solution.py:112
  163.8 319.0 %all-reduce.2.cloned.1.call-start = ((), (), s32[]{:S(2)}) async-start(), calls=%async_computation.7 | async-start | bytes 262144 | tf_op jit(solution)/shard_map/psum | solution.py:120
Sparse Core Ops, SparseCore 0:
  35.8 95.2 all-gather.1
  163.9 128.5 reduce-scatter.1
  295.4 187.3 all-reduce.1
where the time goes:
time: 492 us; the launch traced here: 491 us
  waiting for transfers between devices  359 us (73%)
  blocking collectives  58.8 us (12%)
  starting transfers between devices  24.1 us (5%)
  matrix products  19.4 us (4%)
  between operations  13.9 us (3%)
  local copies, waits for them, and re-layouts  9.41 us (2%)
  other arithmetic  6.86 us (1%)
    psum x1, waiting for transfers between devices, local(): qk_grad = lax.psum(shard_sum, 'group').astype(jnp.float32)  188 us
    reduce_scatter x1, waiting for transfers between devices, local(): lax.psum_scatter(jnp.einsum('td,tk->dk', hidden, q_grad, preferred_elemen...  63.8 us
    all_to_all x1, blocking collectives, local(): lax.all_to_all(slot_values, 'shard', split_axis=0, concat_axis=0, tiled=T...  58.8 us
    all_to_all x1, waiting for transfers between devices, local(): lax.all_to_all(send_grad, 'shard', split_axis=0, concat_axis=0, tiled=True)  53 us
    all_to_all x1, waiting for transfers between devices, local(): lax.all_to_all(send_feat, 'shard', split_axis=0, concat_axis=0, tiled=True)  51.1 us
  transfers between devices with their start and end apart: 6, of which 5 were waited for; matrix products, arithmetic and copies ran while one was open for 5% of the time, Pallas kernels for 0%

commit v1 on v0

v1 whole, which is shorter than its diff:
```python
import functools
import math

import jax
import jax.numpy as jnp
from jax import lax
from jax.experimental import pallas as pl
from jax.experimental.pallas import tpu as pltpu
from jax.sharding import PartitionSpec as P

NX = 4
HEAD = 128
TOK = 64
BLOCK = 128
MESH = pl.DeviceIdType.MESH
F32 = jnp.float32
BF16 = jnp.bfloat16


def dot(a, b, dims=((1,), (0,))):
    return lax.dot_general(a, b, (dims, ((), ())), preferred_element_type=F32)


def iota(shape, dim):
    return lax.broadcasted_iota(jnp.int32, shape, dim)


def pool_kernel(n_owner, per_step, owners, clusters, feat, grad, part, cnt, acc):
    step = pl.program_id(0)

    @pl.when(step == 0)
    def _():
        acc[...] = jnp.zeros_like(acc)
        cnt[...] = jnp.zeros_like(cnt)

    ones = jnp.ones((8, BLOCK), BF16)
    for i in range(per_step):
        owner = owners[step * per_step + i]
        slot = (owner % 2) * (n_owner // 2) + ((owner // 2) % 2) * (n_owner // 4) + owner // 4
        labels = clusters[pl.ds(i, 1), :]
        member = (iota((BLOCK, BLOCK), 0) == labels).astype(F32).astype(BF16)
        rows = pl.ds(i * BLOCK, BLOCK)
        both = jnp.concatenate([feat[rows, :], grad[rows, :]], axis=1)
        acc[slot] += dot(member[:TOK], both)
        cnt[owner // 4, pl.ds(owner % 4, 1), :] += dot(ones, member, ((1,), (1,)))[:1]

    @pl.when(step == pl.num_programs(0) - 1)
    def _():
        for k in range(n_owner):
            part[k] = acc[k].astype(BF16)


def pool(owners, clusters, feat, grad, n_owner):
    nb = owners.shape[0]
    per_step = 8
    return pl.pallas_call(
        functools.partial(pool_kernel, n_owner, per_step),
        out_shape=(
            jax.ShapeDtypeStruct((n_owner, TOK, 2 * BLOCK), BF16),
            jax.ShapeDtypeStruct((n_owner // 4, 8, BLOCK), F32),
        ),
        grid=(nb // per_step,),
        in_specs=[
            pl.BlockSpec(memory_space=pltpu.SMEM),
            pl.BlockSpec((per_step, BLOCK), lambda i: (i, 0)),
            pl.BlockSpec((per_step * BLOCK, BLOCK), lambda i: (i, 0)),
            pl.BlockSpec((per_step * BLOCK, BLOCK), lambda i: (i, 0)),
        ],
        out_specs=(
            pl.BlockSpec((n_owner, TOK, 2 * BLOCK), lambda i: (0, 0, 0)),
            pl.BlockSpec((n_owner // 4, 8, BLOCK), lambda i: (0, 0, 0)),
        ),
        scratch_shapes=[pltpu.VMEM((n_owner, TOK, 2 * BLOCK), F32)],
    )(owners, clusters, feat, grad)


def unpool_kernel(per_step, owners, clusters, feat, table, out):
    step = pl.program_id(0)
    for i in range(per_step):
        owner = owners[step * per_step + i]
        labels = clusters[pl.ds(i, 1), :]
        member = (iota((TOK, BLOCK), 0) == labels).astype(F32).astype(BF16)
        rows = pl.ds(i * BLOCK, BLOCK)
        picked = dot(member, table[owner], ((0,), (0,)))
        out[rows, :] = (feat[rows, :].astype(F32) + picked).astype(BF16)


def unpool(owners, clusters, feat, table):
    nb = owners.shape[0]
    per_step = 8
    return pl.pallas_call(
        functools.partial(unpool_kernel, per_step),
        out_shape=jax.ShapeDtypeStruct(feat.shape, BF16),
        grid=(nb // per_step,),
        in_specs=[
            pl.BlockSpec(memory_space=pltpu.SMEM),
            pl.BlockSpec((per_step, BLOCK), lambda i: (i, 0)),
            pl.BlockSpec((per_step * BLOCK, BLOCK), lambda i: (i, 0)),
            pl.BlockSpec(table.shape, lambda i: (0, 0, 0)),
        ],
        out_specs=pl.BlockSpec((per_step * BLOCK, BLOCK), lambda i: (i, 0)),
    )(owners, clusters, feat, table)


def layer_kernel(
    nx, nzh, ny, n_sem,
    part, cnt, w, tok, w_in, w_out,
    table_out, fin_out,
    pc, ps1, pz, ps2, py, cy, c1, cr, c2, cq, wb, tk, pl4, hid, up, ur, ub,
    ga, gb, gca, gcb, gsa, gsb, gya, gzb, ra, rb, qa, qb, fz, fx,
    send, recv,
):
    g = lax.axis_index("group")
    s = lax.axis_index("shard")
    x = g // nzh
    zh = g % nzh
    y = s // 4
    z = (s // 2) % 2
    c = s % 2
    zc = s % 4
    nz = 2 * nzh
    zz = zh * 2 + z
    d = hid.shape[1]
    cols = 2 * HEAD
    quarter = TOK // nzh

    core = (g, s + 1 - 2 * c)
    zpair = (g, s + 2 - 4 * z)

    def ydev(o):
        return (g, ((y + o) % ny) * 4 + zc)

    def xdev(o):
        return (((x + o) % nx) * nzh + zh, s)

    def zdev(o):
        t = (zz + o) % nz
        return (x * nzh + t // 2, y * 4 + (t % 2) * 2 + c)

    def zhdev(o):
        return (x * nzh + (zh + o) % nzh, s)

    used = []

    def copy(src, dst, dev):
        i = len(used)
        assert i < n_sem
        r = pltpu.make_async_remote_copy(
            src_ref=src, dst_ref=dst, send_sem=send.at[i], recv_sem=recv.at[i],
            device_id=dev, device_id_type=MESH,
        )
        used.append(r)
        r.start()
        return r

    peers = [core] + [ydev(o) for o in range(1, ny)] + [xdev(o) for o in range(1, nx)]
    peers += [zdev(o) for o in range(1, nz)]
    barrier = pltpu.get_barrier_semaphore()
    for dev in peers:
        pl.semaphore_signal(barrier, inc=1, device_id=dev, device_id_type=MESH)
    pl.semaphore_wait(barrier, len(peers))

    first = copy(part.at[1 - c, 1 - z], pc.at[1 - z], core)
    second = copy(part.at[1 - c, z], pc.at[z], core)
    counts_y = [copy(cnt.at[(y + o) % ny], cy.at[y], ydev(o)) for o in range(1, ny)]
    mine = pl.ds(pl.multiple_of(x * cols, cols), cols)
    w_y = [copy(w.at[:, mine], wb.at[y, zc], ydev(o)) for o in range(1, ny)]
    tok_x = [copy(tok, tk.at[x], xdev(o)) for o in range(1, nx)]
    wb[y, zc] = w[:, mine]
    tk[x] = tok[...]

    first.wait_recv()
    for k in range(ny):
        ps1[k] = (part[c, 1 - z, k].astype(F32) + pc[1 - z, k].astype(F32)).astype(BF16)
    pool_z = copy(ps1, pz, zpair)

    total = cnt[y]
    for o, r in enumerate(counts_y):
        r.wait_recv()
        total = total + cy[(y + ny - o - 1) % ny]
    c1[...] = total
    counts_c = copy(c1, cr, core)

    for r in w_y:
        r.wait_recv()
    w_z = copy(wb.at[:, zc], wb.at[:, zc], zpair)
    w_c1 = copy(wb.at[:, zc], wb.at[:, zc], core)

    counts_c.wait_recv()
    c2[...] = c1[...] + cr[...]
    counts_z = copy(c2, cq, zpair)

    second.wait_recv()
    pool_z.wait_recv()
    for k in range(ny):
        ps2[k] = (
            part[c, z, k].astype(F32) + pc[z, k].astype(F32) + pz[k].astype(F32)
        ).astype(BF16)
    pool_y = [copy(ps2.at[(y + o) % ny], py.at[y], ydev(o)) for o in range(1, ny)]

    w_z.wait_recv()
    zc_far = (1 - z) * 2 + c
    w_c2 = copy(wb.at[:, zc_far], wb.at[:, zc_far], core)

    counts_z.wait_recv()
    count = c2[...] + cq[...]
    row = jnp.sum(jnp.where(iota(count.shape, 0) == zc, count, 0.0), axis=0, keepdims=True)
    eye = iota((TOK, HEAD), 0) == iota((TOK, HEAD), 1)
    column = jnp.sum(jnp.where(eye, jnp.broadcast_to(row, (TOK, HEAD)), 0.0), axis=1, keepdims=True)

    sums = ps2[y].astype(F32)
    for o, r in enumerate(pool_y):
        r.wait_recv()
        sums = sums + py[(y + ny - o - 1) % ny].astype(F32)
    pl4[x, :, 0:HEAD] = (sums[:, :HEAD] / jnp.maximum(column, 1.0)).astype(BF16)
    pl4[x, :, HEAD : 2 * HEAD] = sums[:, HEAD:].astype(BF16)
    pool_x = [copy(pl4.at[x], pl4.at[x], xdev(o)) for o in range(1, nx)]

    for r in tok_x:
        r.wait_recv()
    w_c1.wait_recv()
    w_c2.wait_recv()
    for r in pool_x:
        r.wait_recv()

    rows = nx * TOK
    pooled = pl4[:, :, 0:HEAD].reshape(rows, HEAD)
    pooled_grad = pl4[:, :, HEAD : 2 * HEAD].reshape(rows, HEAD)
    step = 512
    for n in range(0, d, step):
        span = slice(n, n + step)
        wide = tk[:, :, span].reshape(rows, step).astype(F32) + dot(pooled, w_in[:, span])
        hid[:, span] = wide.astype(BF16)
    queries = dot(hid[...], wb[...].reshape(d, cols)).astype(BF16)
    head_rows = pl.ds(pl.multiple_of(x * cols, cols), cols)
    tail_rows = pl.ds(pl.multiple_of(nx * cols + x * cols, cols), cols)
    out_grad = dot(pooled_grad, w_out[head_rows, :], ((1,), (1,))).astype(BF16)
    values = hid[:, head_rows]
    scale = 1.0 / math.sqrt(HEAD)
    pair = 2 * TOK
    ii, jj = iota((pair, pair), 0), iota((pair, pair), 1)
    same = (ii // TOK) == (jj // TOK)
    diag = ii == jj
    out_parts, q_parts = [], []
    for p in range(rows // pair):
        ps = slice(p * pair, (p + 1) * pair)
        out_row, q_row = [], []
        for h in range(2):
            hs = slice(h * HEAD, (h + 1) * HEAD)
            q, v, og = queries[ps, hs], values[ps, hs], out_grad[ps, hs]
            scores = dot(q, q, ((1,), (1,))) * scale
            scores = jnp.where(diag, -1000000000.0, scores)
            scores = jnp.where(same, scores, -jnp.inf)
            e = jnp.exp(scores - jnp.max(scores, axis=1, keepdims=True))
            prob = e / jnp.sum(e, axis=1, keepdims=True)
            attended = dot(prob.astype(BF16), v)
            out_row.append((v.astype(F32) + attended).astype(BF16))
            prob_grad = dot(og, v, ((1,), (1,)))
            inner = jnp.sum(prob_grad * prob, axis=1, keepdims=True)
            score_grad = (prob * (prob_grad - inner) * scale).astype(BF16)
            q_row.append((dot(score_grad, q) + dot(score_grad, q, ((0,), (0,)))).astype(BF16))
        out_parts.append(jnp.concatenate(out_row, axis=1))
        q_parts.append(jnp.concatenate(q_row, axis=1))
    out_cols = jnp.concatenate(out_parts, axis=0)
    q_grad = jnp.concatenate(q_parts, axis=0)
    unp = dot(out_cols, w_out[head_rows, :]) + dot(hid[:, tail_rows], w_out[tail_rows, :])
    unp = unp.astype(BF16)
    for k in range(nx):
        up[k] = unp[k * TOK : (k + 1) * TOK]
    unp_x = [copy(up.at[(x + o) % nx], ur.at[x], xdev(o)) for o in range(1, nx)]

    for k in range(2 * ny):
        yk, zk = k // 2, k % 2
        term = dot(hid[:, 2 * TOK * k : 2 * TOK * (k + 1)], q_grad, ((0,), (0,))).astype(BF16)
        for ck in range(2):
            ga[ck, yk, zk] = term[TOK * ck : TOK * (ck + 1), :HEAD]
            for q in range(nzh):
                at = TOK * ck + quarter * q
                gb[ck, zk, q, yk] = term[at : at + quarter, HEAD:]
    grad_a = copy(ga.at[1 - c], gca, core)
    grad_b = copy(gb.at[1 - c], gcb, core)

    sums = up[x].astype(F32)
    for o, r in enumerate(unp_x):
        r.wait_recv()
        sums = sums + ur[(x + nx - o - 1) % nx].astype(F32)
    ub[y, zc] = sums.astype(BF16)
    unp_y = [copy(ub.at[y, zc], ub.at[y, zc], ydev(o)) for o in range(1, ny)]

    grad_a.wait_recv()
    for k in range(ny):
        gsa[k] = (ga[c, k].astype(F32) + gca[k].astype(F32)).astype(BF16)
    ga_y = [copy(gsa.at[(y + o) % ny], gya.at[y], ydev(o)) for o in range(1, ny)]
    grad_b.wait_recv()
    for zk in range(2):
        for q in range(nzh):
            gsb[zk, q] = (gb[c, zk, q].astype(F32) + gcb[zk, q].astype(F32)).astype(BF16)

    def zslot(o):
        t = (zz + o) % nz
        return t % 2, t // 2

    gb_z = [copy(gsb.at[zslot(o)], gzb.at[zz], zdev(o)) for o in range(1, nz)]

    for r in unp_y:
        r.wait_recv()
    unp_z = copy(ub.at[:, zc], ub.at[:, zc], zpair)
    unp_c1 = copy(ub.at[:, zc], ub.at[:, zc], core)

    sums = gsa[y].astype(F32)
    for o, r in enumerate(ga_y):
        r.wait_recv()
        sums = sums + gya[(y + ny - o - 1) % ny].astype(F32)
    for zk in range(2):
        for q in range(nzh):
            ra[zk, q] = sums[zk, quarter * q : quarter * (q + 1)].astype(BF16)
    qa_z = [copy(ra.at[zslot(o)], qa.at[zz], zdev(o)) for o in range(1, nz)]
    sums = gsb[z, zh].astype(F32)
    for o, r in enumerate(gb_z):
        r.wait_recv()
        sums = sums + gzb[(zz + nz - o - 1) % nz].astype(F32)
    rb[...] = sums.astype(BF16)
    qb_y = [copy(rb.at[(y + o) % ny], qb.at[y], ydev(o)) for o in range(1, ny)]

    unp_z.wait_recv()
    unp_c2 = copy(ub.at[:, zc_far], ub.at[:, zc_far], core)

    sums = ra[z, zh].astype(F32)
    for o, r in enumerate(qa_z):
        r.wait_recv()
        sums = sums + qa[(zz + nz - o - 1) % nz].astype(F32)
    fz[zh, :, 0:HEAD] = sums.astype(BF16)
    sums = rb[y].astype(F32)
    for o, r in enumerate(qb_y):
        r.wait_recv()
        sums = sums + qb[(y + ny - o - 1) % ny].astype(F32)
    fz[zh, :, HEAD : 2 * HEAD] = sums.astype(BF16)
    fin_z = [copy(fz.at[zh], fz.at[zh], zhdev(o)) for o in range(1, nzh)]

    unp_c1.wait_recv()
    unp_c2.wait_recv()
    table_out[...] = ub[...].reshape(table_out.shape)

    for r in fin_z:
        r.wait_recv()
    fin_x = [copy(fz, fx.at[x], xdev(o)) for o in range(1, nx)]
    fx[x] = fz[...]
    for r in fin_x:
        r.wait_recv()
    for k in range(nx):
        fin_out[:, cols * k : cols * (k + 1)] = fx[k].reshape(TOK, cols).astype(F32)
    for r in used:
        r.wait_send()


def layer(part, cnt, w, tok, w_in, w_out, nzh, ny):
    nx, nz = NX, 2 * nzh
    d = w_in.shape[1]
    cols = 2 * HEAD
    quarter = TOK // nzh
    n_sem = 2 + 7 * (ny - 1) + 4 * (nx - 1) + 2 * (nz - 1) + (nzh - 1) + 13
    v = lambda *shape: pltpu.VMEM(shape, BF16)
    vf = lambda *shape: pltpu.VMEM(shape, F32)
    scratch = [
        v(2, ny, TOK, cols), v(ny, TOK, cols), v(ny, TOK, cols), v(ny, TOK, cols), v(ny, TOK, cols),
        vf(ny, 8, HEAD), vf(8, HEAD), vf(8, HEAD), vf(8, HEAD), vf(8, HEAD),
        v(ny, 4, TOK, cols), v(nx, TOK, d), v(nx, TOK, cols), v(nx * TOK, d),
        v(nx, TOK, HEAD), v(nx, TOK, HEAD), v(ny, 4, TOK, HEAD),
        v(2, ny, 2, TOK, HEAD), v(2, 2, nzh, ny, quarter, HEAD),
        v(ny, 2, TOK, HEAD), v(2, nzh, ny, quarter, HEAD),
        v(ny, 2, TOK, HEAD), v(2, nzh, ny, quarter, HEAD),
        v(ny, 2, TOK, HEAD), v(nz, ny, quarter, HEAD),
        v(2, nzh, quarter, HEAD), v(ny, quarter, HEAD), v(nz, quarter, HEAD), v(ny, quarter, HEAD),
        v(nzh, quarter, cols), v(nx, nzh, quarter, cols),
        pltpu.SemaphoreType.DMA((n_sem,)), pltpu.SemaphoreType.DMA((n_sem,)),
    ]
    vmem = pl.BlockSpec(memory_space=pltpu.VMEM)
    return pl.pallas_call(
        functools.partial(layer_kernel, nx, nzh, ny, n_sem),
        out_shape=(
            jax.ShapeDtypeStruct((4 * ny, TOK, HEAD), BF16),
            jax.ShapeDtypeStruct((TOK, nx * cols), F32),
        ),
        in_specs=[vmem] * 6,
        out_specs=(vmem, vmem),
        scratch_shapes=scratch,
        compiler_params=pltpu.CompilerParams(collective_id=0, has_side_effects=True),
    )(part, cnt, w, tok, w_in, w_out)


def local(tokens, w_qk, w_in, w_out, particles, cotangent, clusters, owners):
    n_shard = lax.axis_size("shard")
    nzh = lax.axis_size("group") // NX
    ny = n_shard // 4
    labels = clusters.reshape(-1, BLOCK)
    part, cnt = pool(owners, labels, particles, cotangent, n_shard)
    part = part.reshape(2, 2, ny, TOK, 2 * HEAD)
    table, qk_grad = layer(part, cnt, w_qk, tokens, w_in, w_out, nzh, ny)
    particle_out = unpool(owners, labels, particles, table)
    return (particle_out, qk_grad)


def solution(mesh):
    placed = (
        P(("group", "shard"), None),
        P("shard", None),
        P(),
        P(),
        P(("group", "shard"), None),
        P(("group", "shard"), None),
        P(("group", "shard")),
        P(("group", "shard")),
    )
    return jax.shard_map(
        local,
        mesh=mesh,
        in_specs=placed,
        out_specs=(P(("group", "shard"), None), P("shard", None)),
        check_vma=False,
    )
```

time: 492 us -> 80.1 us (0.16)
  the two profiles are of different devices: /device:TPU:16 before, /device:TPU:64 now
where the time goes in v1:
time: 80.1 us; the launch traced here: 79.8 us
  Pallas kernels  78.5 us (98%)
    pallas_call x1, Pallas kernels, layer(): pl.pallas_call(functools.partial(layer_kernel, nx, nzh, ny, n_sem), out_s...  69.9 us
    pallas_call x1, Pallas kernels, pool(): pl.pallas_call(functools.partial(pool_kernel, n_owner, per_step), out_sha...  4.47 us
    pallas_call x1, Pallas kernels, unpool(): pl.pallas_call(functools.partial(unpool_kernel, per_step), out_shape=jax....  4.13 us

profile of v1, /device:TPU:64, one launch (start us, length us, event | category | flops | bytes accessed | tf_op | source)
XLA Modules:
  0.0 79.8 jit_solution(16448833781274306282)
XLA Ops:
  0.6 4.5 %shard_map.95 = (bf16[32,64,256]{2,1,0:T(8,128)(2,1)}, f32[8,8,128]{2,1,0:T(8,128)}) custom-call(s32[32]{0:T(128)} %owners.3, s32[32,128]{1,0:T(8,128)} %bitcast.3, bf16[4096,128]{1,0:T(8,128)(2,1)} %feat.3, bf16[4096,128]{1,0:T(8,128)(2,1)} %grad.1), custom_call_target="tpu_custom_call" | custom-call | tf_op jit(solution)/shard_map/pallas_call | solution.py:56
  5.1 69.9 %shard_map.96 = (bf16[32,64,128]{2,1,0:T(8,128)(2,1)}, f32[64,1024]{1,0:T(8,128)}) custom-call(bf16[2,2,8,64,256]{4,3,2,1,0:T(8,128)(2,1)} %bitcast.2, f32[8,8,128]{2,1,0:T(8,128)} %get-tuple-element.7.cnt, bf16[64,1024]{1,0:T(8,128)(2,1)} %w.1, bf16[64,2048]{1,0:T(8,128)(2,1)} %tok.1, bf16[128,2048]{1,0:T(8,128)(2,1)} %w_in.1, bf16[2048,128]{1,0:T(8,128)(2,1)} %w_out.1), custom_call_target="tpu_custom_call" | custom-call | tf_op jit(solution)/shard_map/pallas_call | solution.py:378
  75.0 0.0 copy-start
  75.0 4.1 %shard_map.97 = bf16[4096,128]{1,0:T(8,128)(2,1)} custom-call(s32[32]{0:T(128)} %owners.3, s32[32,128]{1,0:T(8,128)} %bitcast.4, bf16[4096,128]{1,0:T(8,128)(2,1)} %feat.3, bf16[32,64,128]{2,1,0:T(8,128)(2,1)} %get-tuple-element.8.table), custom_call_target="tpu_custom_call" | custom-call | tf_op jit(solution)/shard_map/pallas_call | solution.py:91
  79.1 0.0 copy-done
  79.1 0.7 copy.11
Async XLA Ops:
  75.0 4.1 %copy-start = (f32[64,1024]{1,0:T(8,128)S(1)}, f32[64,1024]{1,0:T(8,128)}, u32[]{:S(2)}) copy-start(f32[64,1024]{1,0:T(8,128)} %get-tuple-element.13) | copy-start | bytes 786436

commit v2 on v1

v2 whole, which is shorter than its diff:
```python
import functools
import math

import jax
import jax.numpy as jnp
from jax import lax
from jax.experimental import pallas as pl
from jax.experimental.pallas import tpu as pltpu
from jax.sharding import PartitionSpec as P

NX = 4
HEAD = 128
TOK = 64
BLOCK = 128
MESH = pl.DeviceIdType.MESH
F32 = jnp.float32
BF16 = jnp.bfloat16


def dot(a, b, dims=((1,), (0,))):
    return lax.dot_general(a, b, (dims, ((), ())), preferred_element_type=F32)


def iota(shape, dim):
    return lax.broadcasted_iota(jnp.int32, shape, dim)


def layer_kernel(
    nx, nzh, ny, n_sem,
    owners, first, last, clusters, w, tok, w_in_hbm, w_out_hbm, feat_hbm, cot_hbm,
    p_out, fin_out,
    fv, cv, w_in, w_out, ob, cnt,
    pf, pg, pcf, pcg, fown, gown, fzs, fzr, gzs, gzr, fys, fyr, gys, gyr,
    cy, c1, cr, c2, cq, wb, tk, plf, plg, hid, up, ur, ub,
    ga, gb, gca, gcb, gsa, gsb, gya, gzb, ra, rb, qa, qb, fx,
    send, recv, here,
):
    g = lax.axis_index("group")
    s = lax.axis_index("shard")
    x = g // nzh
    zh = g % nzh
    y = s // 4
    z = (s // 2) % 2
    c = s % 2
    zc = s % 4
    zc_far = (1 - z) * 2 + c
    nz = 2 * nzh
    zz = zh * 2 + z
    d = hid.shape[1]
    cols = 2 * HEAD
    quarter = TOK // nzh
    nb = owners.shape[0]

    core = (g, s + 1 - 2 * c)
    zpair = (g, s + 2 - 4 * z)

    def ydev(o):
        return (g, ((y + o) % ny) * 4 + zc)

    def xdev(o):
        return (((x + o) % nx) * nzh + zh, s)

    def zslot(o):
        t = (zz + o) % nz
        return t % 2, t // 2

    def zdev(o):
        zo, zho = zslot(o)
        return (x * nzh + zho, y * 4 + zo * 2 + c)

    def xzdev(ox, oz):
        return (((x + ox) % nx) * nzh + (zh + oz) % nzh, s)

    xz = [(ox, oz) for ox in range(nx) for oz in range(nzh) if ox or oz]
    used = []

    def copy(src, dst, dev):
        i = len(used)
        assert i < n_sem
        r = pltpu.make_async_remote_copy(
            src_ref=src, dst_ref=dst, send_sem=send.at[i], recv_sem=recv.at[i],
            device_id=dev, device_id_type=MESH,
        )
        used.append(r)
        r.start()
        return r

    peers = [core] + [ydev(o) for o in range(1, ny)] + [zdev(o) for o in range(1, nz)]
    peers += [xzdev(ox, oz) for ox, oz in xz if ox]
    barrier = pltpu.get_barrier_semaphore()
    for dev in peers:
        pl.semaphore_signal(barrier, inc=1, device_id=dev, device_id_type=MESH)
    mine = pl.ds(pl.multiple_of(x * cols, cols), cols)
    loads = [
        pltpu.make_async_copy(feat_hbm, fv, here.at[0]),
        pltpu.make_async_copy(cot_hbm, cv, here.at[1]),
        pltpu.make_async_copy(w.at[:, mine], wb.at[y, zc], here.at[2]),
        pltpu.make_async_copy(tok, tk.at[x], here.at[3]),
        pltpu.make_async_copy(w_in_hbm, w_in, here.at[4]),
        pltpu.make_async_copy(w_out_hbm, w_out, here.at[5]),
    ]
    for r in loads:
        r.start()
    cnt[...] = jnp.zeros_like(cnt)
    pl.semaphore_wait(barrier, len(peers))

    w_y = [copy(w.at[:, mine], wb.at[y, zc], ydev(o)) for o in range(1, ny)]
    tok_x = [copy(tok, tk.at[x], xdev(o)) for o in range(1, nx)]

    ones = jnp.ones((8, 2 * BLOCK), BF16)

    def pooled_sum(yk, zk, ck):
        owner = yk * 4 + zk * 2 + ck
        member, feats, cots = [], [], []
        b0, b1 = first[owner], last[owner]
        for at, valid in ((jnp.minimum(b0, nb - 1), b0 < nb), (jnp.maximum(b1, 0), b1 > b0)):
            labels = jnp.where(valid, clusters[pl.ds(at, 1), :], -1)
            member.append((iota((TOK, BLOCK), 0) == labels).astype(F32).astype(BF16))
            feats.append(fv[at])
            cots.append(cv[at])
        member = jnp.concatenate(member, axis=1)
        both = jnp.concatenate(
            [jnp.concatenate(feats, axis=0), jnp.concatenate(cots, axis=0)], axis=1
        )
        cnt[yk, pl.ds(zk * 2 + ck, 1), 0:TOK] = dot(ones, member, ((1,), (1,)))[:1]
        return dot(member, both)

    loads[0].wait()
    loads[1].wait()
    for yk in range(ny):
        for zk in range(2):
            v = pooled_sum(yk, zk, 1 - c)
            pf[zk, yk] = v[:, :HEAD].astype(BF16)
            pg[zk, yk] = v[:, HEAD:].astype(BF16)
    pool_f = copy(pf, pcf, core)
    pool_g = copy(pg, pcg, core)
    for yk in range(ny):
        for zk in range(2):
            v = pooled_sum(yk, zk, c)
            fown[zk, yk] = v[:, :HEAD]
            gown[zk, yk] = v[:, HEAD:]
    counts_y = [copy(cnt.at[(y + o) % ny], cy.at[y], ydev(o)) for o in range(1, ny)]

    pool_f.wait_recv()
    for k in range(ny):
        fzs[k] = (fown[1 - z, k] + pcf[1 - z, k].astype(F32)).astype(BF16)
    feat_z = copy(fzs, fzr, zpair)
    pool_g.wait_recv()
    for k in range(ny):
        gzs[k] = (gown[1 - z, k] + pcg[1 - z, k].astype(F32)).astype(BF16)
    cot_z = copy(gzs, gzr, zpair)

    feat_z.wait_recv()
    for k in range(ny):
        fys[k] = (fown[z, k] + pcf[z, k].astype(F32) + fzr[k].astype(F32)).astype(BF16)
    feat_y = [copy(fys.at[(y + o) % ny], fyr.at[y], ydev(o)) for o in range(1, ny)]

    total = cnt[y]
    for o, r in enumerate(counts_y):
        r.wait_recv()
        total = total + cy[(y + ny - o - 1) % ny]
    c1[...] = total
    counts_c = copy(c1, cr, core)

    for r in w_y:
        r.wait_recv()
    loads[2].wait()
    w_z = copy(wb.at[:, zc], wb.at[:, zc], zpair)
    w_c1 = copy(wb.at[:, zc], wb.at[:, zc], core)

    counts_c.wait_recv()
    c2[...] = c1[...] + cr[...]
    counts_z = copy(c2, cq, zpair)

    cot_z.wait_recv()
    for k in range(ny):
        gys[k] = (gown[z, k] + pcg[z, k].astype(F32) + gzr[k].astype(F32)).astype(BF16)
    cot_y = [copy(gys.at[(y + o) % ny], gyr.at[y], ydev(o)) for o in range(1, ny)]

    counts_z.wait_recv()
    count = c2[...] + cq[...]
    row = jnp.sum(jnp.where(iota(count.shape, 0) == zc, count, 0.0), axis=0, keepdims=True)
    eye = iota((TOK, HEAD), 0) == iota((TOK, HEAD), 1)
    column = jnp.sum(jnp.where(eye, jnp.broadcast_to(row, (TOK, HEAD)), 0.0), axis=1, keepdims=True)

    sums = fys[y].astype(F32)
    for o, r in enumerate(feat_y):
        r.wait_recv()
        sums = sums + fyr[(y + ny - o - 1) % ny].astype(F32)
    plf[x] = (sums / jnp.maximum(column, 1.0)).astype(BF16)
    feat_x = [copy(plf.at[x], plf.at[x], xdev(o)) for o in range(1, nx)]

    sums = gys[y].astype(F32)
    for o, r in enumerate(cot_y):
        r.wait_recv()
        sums = sums + gyr[(y + ny - o - 1) % ny].astype(F32)
    plg[x] = sums.astype(BF16)
    cot_x = [copy(plg.at[x], plg.at[x], xdev(o)) for o in range(1, nx)]

    for r in loads[3:]:
        r.wait()
    for r in tok_x:
        r.wait_recv()
    for r in feat_x:
        r.wait_recv()

    rows = nx * TOK
    pooled = plf[...].reshape(rows, HEAD)
    step = 512
    for n in range(0, d, step):
        span = slice(n, n + step)
        wide = tk[:, :, span].reshape(rows, step).astype(F32) + dot(pooled, w_in[:, span])
        hid[:, span] = wide.astype(BF16)
    w_z.wait_recv()
    w_c2 = copy(wb.at[:, zc_far], wb.at[:, zc_far], core)
    w_c1.wait_recv()
    w_c2.wait_recv()
    queries = dot(hid[...], wb[...].reshape(d, cols)).astype(BF16)
    head_rows = pl.ds(pl.multiple_of(x * cols, cols), cols)
    tail_rows = pl.ds(pl.multiple_of(nx * cols + x * cols, cols), cols)
    values = hid[:, head_rows]
    scale = 1.0 / math.sqrt(HEAD)
    pair = 2 * TOK
    ii, jj = iota((pair, pair), 0), iota((pair, pair), 1)
    same = (ii // TOK) == (jj // TOK)
    diag = ii == jj
    probs, out_parts = {}, []
    for p in range(rows // pair):
        ps = slice(p * pair, (p + 1) * pair)
        out_row = []
        for h in range(2):
            hs = slice(h * HEAD, (h + 1) * HEAD)
            q, v = queries[ps, hs], values[ps, hs]
            scores = dot(q, q, ((1,), (1,))) * scale
            scores = jnp.where(diag, -1000000000.0, scores)
            scores = jnp.where(same, scores, -jnp.inf)
            e = jnp.exp(scores - jnp.max(scores, axis=1, keepdims=True))
            prob = e / jnp.sum(e, axis=1, keepdims=True)
            probs[p, h] = prob
            attended = dot(prob.astype(BF16), v)
            out_row.append((v.astype(F32) + attended).astype(BF16))
        out_parts.append(jnp.concatenate(out_row, axis=1))
    out_cols = jnp.concatenate(out_parts, axis=0)
    unp = dot(out_cols, w_out[head_rows, :]) + dot(hid[:, tail_rows], w_out[tail_rows, :])
    unp = unp.astype(BF16)
    for k in range(nx):
        up[k] = unp[k * TOK : (k + 1) * TOK]
    unp_x = [copy(up.at[(x + o) % nx], ur.at[x], xdev(o)) for o in range(1, nx)]

    for r in cot_x:
        r.wait_recv()
    pooled_grad = plg[...].reshape(rows, HEAD)
    out_grad = dot(pooled_grad, w_out[head_rows, :], ((1,), (1,))).astype(BF16)
    q_parts = []
    for p in range(rows // pair):
        ps = slice(p * pair, (p + 1) * pair)
        q_row = []
        for h in range(2):
            hs = slice(h * HEAD, (h + 1) * HEAD)
            q, v, prob = queries[ps, hs], values[ps, hs], probs[p, h]
            prob_grad = dot(out_grad[ps, hs], v, ((1,), (1,)))
            inner = jnp.sum(prob_grad * prob, axis=1, keepdims=True)
            score_grad = (prob * (prob_grad - inner) * scale).astype(BF16)
            q_row.append((dot(score_grad, q) + dot(score_grad, q, ((0,), (0,)))).astype(BF16))
        q_parts.append(jnp.concatenate(q_row, axis=1))
    q_grad = jnp.concatenate(q_parts, axis=0)

    grad_b = []
    for zk in range(2):
        for yk in range(ny):
            k = yk * 2 + zk
            term = dot(hid[:, 2 * TOK * k : 2 * TOK * (k + 1)], q_grad, ((0,), (0,))).astype(BF16)
            for ck in range(2):
                ga[ck, yk, zk] = term[TOK * ck : TOK * (ck + 1), :HEAD]
                for q in range(nzh):
                    at = TOK * ck + quarter * q
                    gb[ck, zk, q, yk] = term[at : at + quarter, HEAD:]
        grad_b.append(copy(gb.at[1 - c, zk], gcb.at[zk], core))
    grad_a = copy(ga.at[1 - c], gca, core)

    sums = up[x].astype(F32)
    for o, r in enumerate(unp_x):
        r.wait_recv()
        sums = sums + ur[(x + nx - o - 1) % nx].astype(F32)
    ub[y, zc] = sums.astype(BF16)
    unp_y = [copy(ub.at[y, zc], ub.at[y, zc], ydev(o)) for o in range(1, ny)]

    for zk in range(2):
        grad_b[zk].wait_recv()
        for q in range(nzh):
            gsb[zk, q] = (gb[c, zk, q].astype(F32) + gcb[zk, q].astype(F32)).astype(BF16)
    gb_z = [copy(gsb.at[zslot(o)], gzb.at[zz], zdev(o)) for o in range(1, nz)]
    grad_a.wait_recv()
    for k in range(ny):
        gsa[k] = (ga[c, k].astype(F32) + gca[k].astype(F32)).astype(BF16)
    ga_y = [copy(gsa.at[(y + o) % ny], gya.at[y], ydev(o)) for o in range(1, ny)]

    for r in unp_y:
        r.wait_recv()
    unp_z = copy(ub.at[:, zc], ub.at[:, zc], zpair)
    unp_c1 = copy(ub.at[:, zc], ub.at[:, zc], core)

    sums = gsb[z, zh].astype(F32)
    for o, r in enumerate(gb_z):
        r.wait_recv()
        sums = sums + gzb[(zz + nz - o - 1) % nz].astype(F32)
    rb[...] = sums.astype(BF16)
    qb_y = [copy(rb.at[(y + o) % ny], qb.at[y], ydev(o)) for o in range(1, ny)]
    sums = gsa[y].astype(F32)
    for o, r in enumerate(ga_y):
        r.wait_recv()
        sums = sums + gya[(y + ny - o - 1) % ny].astype(F32)
    for zk in range(2):
        for q in range(nzh):
            ra[zk, q] = sums[zk, quarter * q : quarter * (q + 1)].astype(BF16)
    qa_z = [copy(ra.at[zslot(o)], qa.at[zz], zdev(o)) for o in range(1, nz)]

    unp_z.wait_recv()
    unp_c2 = copy(ub.at[:, zc_far], ub.at[:, zc_far], core)

    sums = rb[y].astype(F32)
    for o, r in enumerate(qb_y):
        r.wait_recv()
        sums = sums + qb[(y + ny - o - 1) % ny].astype(F32)
    fx[x, zh, :, HEAD : 2 * HEAD] = sums.astype(BF16)
    sums = ra[z, zh].astype(F32)
    for o, r in enumerate(qa_z):
        r.wait_recv()
        sums = sums + qa[(zz + nz - o - 1) % nz].astype(F32)
    fx[x, zh, :, 0:HEAD] = sums.astype(BF16)
    fin = [copy(fx.at[x, zh], fx.at[x, zh], xzdev(ox, oz)) for ox, oz in xz]

    unp_c1.wait_recv()
    unp_c2.wait_recv()
    stores = []
    per = nb // 4
    for b in range(nb):
        owner = owners[b]
        member = (iota((TOK, BLOCK), 0) == clusters[b : b + 1, :]).astype(F32).astype(BF16)
        picked = dot(member, ub[owner // 4, owner % 4], ((0,), (0,)))
        ob[b] = (fv[b].astype(F32) + picked).astype(BF16)
        if b % per == per - 1:
            span = pl.ds(b + 1 - per, per)
            r = pltpu.make_async_copy(ob.at[span], p_out.at[span], here.at[6 + b // per])
            r.start()
            stores.append(r)

    for r in fin:
        r.wait_recv()
    for k in range(nx):
        fin_out[:, cols * k : cols * (k + 1)] = fx[k].reshape(TOK, cols).astype(F32)
    for r in stores:
        r.wait()
    for r in used:
        r.wait_send()


def layer(owners, first, last, clusters, w, tok, w_in, w_out, feat, cot, nzh, ny):
    nx, nz = NX, 2 * nzh
    d = w_in.shape[1]
    cols = 2 * HEAD
    quarter = TOK // nzh
    nb = owners.shape[0]
    n_sem = 20 + 9 * (ny - 1) + 4 * (nx - 1) + 2 * (nz - 1) + nx * nzh
    v = lambda *shape: pltpu.VMEM(shape, BF16)
    vf = lambda *shape: pltpu.VMEM(shape, F32)
    half = (2, ny, TOK, HEAD)
    side = (ny, TOK, HEAD)
    scratch = [
        v(nb, BLOCK, HEAD), v(nb, BLOCK, HEAD), v(*w_in.shape), v(*w_out.shape),
        v(nb, BLOCK, HEAD), vf(ny, 8, HEAD),
        v(*half), v(*half), v(*half), v(*half), vf(*half), vf(*half),
        v(*side), v(*side), v(*side), v(*side), v(*side), v(*side), v(*side), v(*side),
        vf(ny, 8, HEAD), vf(8, HEAD), vf(8, HEAD), vf(8, HEAD), vf(8, HEAD),
        v(ny, 4, TOK, cols), v(nx, TOK, d), v(nx, TOK, HEAD), v(nx, TOK, HEAD), v(nx * TOK, d),
        v(nx, TOK, HEAD), v(nx, TOK, HEAD), v(ny, 4, TOK, HEAD),
        v(2, ny, 2, TOK, HEAD), v(2, 2, nzh, ny, quarter, HEAD),
        v(ny, 2, TOK, HEAD), v(2, nzh, ny, quarter, HEAD),
        v(ny, 2, TOK, HEAD), v(2, nzh, ny, quarter, HEAD),
        v(ny, 2, TOK, HEAD), v(nz, ny, quarter, HEAD),
        v(2, nzh, quarter, HEAD), v(ny, quarter, HEAD), v(nz, quarter, HEAD), v(ny, quarter, HEAD),
        v(nx, nzh, quarter, cols),
        pltpu.SemaphoreType.DMA((n_sem,)), pltpu.SemaphoreType.DMA((n_sem,)),
        pltpu.SemaphoreType.DMA((10,)),
    ]
    vmem = pl.BlockSpec(memory_space=pltpu.VMEM)
    smem = pl.BlockSpec(memory_space=pltpu.SMEM)
    hbm = pl.BlockSpec(memory_space=pl.ANY)
    return pl.pallas_call(
        functools.partial(layer_kernel, nx, nzh, ny, n_sem),
        out_shape=(
            jax.ShapeDtypeStruct((nb, BLOCK, HEAD), BF16),
            jax.ShapeDtypeStruct((TOK, nx * cols), F32),
        ),
        in_specs=[smem, smem, smem, vmem] + [hbm] * 6,
        out_specs=(hbm, vmem),
        scratch_shapes=scratch,
        compiler_params=pltpu.CompilerParams(collective_id=0, has_side_effects=True),
    )(owners, first, last, clusters, w, tok, w_in, w_out, feat, cot)


def local(tokens, w_qk, w_in, w_out, particles, cotangent, clusters, owners):
    n_shard = lax.axis_size("shard")
    nzh = lax.axis_size("group") // NX
    nb = owners.shape[0]
    ids = (n_shard, nb)
    at = iota(ids, 1)
    named = jnp.broadcast_to(owners[None, :], ids) == iota(ids, 0)
    first = jnp.min(jnp.where(named, at, nb), axis=1)
    last = jnp.max(jnp.where(named, at, -1), axis=1)
    feat = particles.reshape(nb, BLOCK, -1)
    cot = cotangent.reshape(nb, BLOCK, -1)
    out, qk_grad = layer(
        owners, first, last, clusters.reshape(nb, BLOCK), w_qk, tokens, w_in, w_out, feat, cot,
        nzh, n_shard // 4,
    )
    return (out.reshape(particles.shape), qk_grad)


def solution(mesh):
    placed = (
        P(("group", "shard"), None),
        P("shard", None),
        P(),
        P(),
        P(("group", "shard"), None),
        P(("group", "shard"), None),
        P(("group", "shard")),
        P(("group", "shard")),
    )
    return jax.shard_map(
        local,
        mesh=mesh,
        in_specs=placed,
        out_specs=(P(("group", "shard"), None), P("shard", None)),
        check_vma=False,
    )
```

time: 80.1 us -> 73.6 us (0.919)
  the two profiles are of different devices: /device:TPU:64 before, /device:TPU:1 now
where the time goes in v2:
time: 73.6 us; the launch traced here: 72.7 us
  Pallas kernels  67.7 us (92%)
  local copies, waits for them, and re-layouts  3.66 us (5%)
    pallas_call x1, Pallas kernels, layer(): pl.pallas_call(functools.partial(layer_kernel, nx, nzh, ny, n_sem), out_s...  67.7 us
    unnamed x6, local copies, waits for them, and re-layouts  3.66 us

profile of v2, /device:TPU:1, one launch (start us, length us, event | category | flops | bytes accessed | tf_op | source)
XLA Modules:
  0.0 72.7 jit_solution(16686997118253684420)
XLA Ops:
  0.6 0.0 copy-start.1
  0.6 0.6 copy-done.1
  1.3 0.6 select_reduce_fusion
  1.9 67.7 %shard_map.95 = (bf16[32,128,128]{2,1,0:T(8,128)(2,1)}, f32[64,1024]{1,0:T(8,128)}) custom-call(s32[32]{0:T(128)} %owners.1, s32[32]{0:T(128)} %get-tuple-element.7.first, s32[32]{0:T(128)} %get-tuple-element.6.last, s32[32,128]{1,0:T(8,128)} %bitcast.7, bf16[64,1024]{1,0:T(8,128)(2,1)} %w.1, bf16[64,2048]{1,0:T(8,128)(2,1)} %tok.1, ...), custom_call_target="tpu_custom_call" | custom-call | tf_op jit(solution)/shard_map/pallas_call | solution.py:389
  69.7 0.0 copy-start
  69.7 2.3 %copy.12 = bf16[4096,128]{1,0:T(8,128)(2,1)} copy(bf16[4096,128]{1,0:T(8,128)(2,1)} %bitcast.4) | data formatting | bytes 2097152
  72.0 0.0 copy-done
  72.0 0.7 copy.13
Async XLA Ops:
  0.6 0.7 copy-start.1
  69.7 2.3 %copy-start = (f32[64,1024]{1,0:T(8,128)S(1)}, f32[64,1024]{1,0:T(8,128)}, u32[]{:S(2)}) copy-start(f32[64,1024]{1,0:T(8,128)} %get-tuple-element.11) | copy-start | bytes 786436

commit v3 on v2

--- a/solution.py
+++ b/solution.py
@@ -29,9 +29,9 @@
     nx, nzh, ny, n_sem,
     owners, first, last, clusters, w, tok, w_in_hbm, w_out_hbm, feat_hbm, cot_hbm,
     p_out, fin_out,
-    fv, cv, w_in, w_out, ob, cnt,
+    fv, cv, w_in, w_out, cnt,
     pf, pg, pcf, pcg, fown, gown, fzs, fzr, gzs, gzr, fys, fyr, gys, gyr,
-    cy, c1, cr, c2, cq, wb, tk, plf, plg, hid, up, ur, ub,
+    cy, c1, cr, c2, cq, wb, tk, plf, plg, hid, hidt, up, ur, ub,
     ga, gb, gca, gcb, gsa, gsb, gya, gzb, ra, rb, qa, qb, fx,
     send, recv, here,
 ):
@@ -165,7 +165,9 @@
     for r in w_y:
         r.wait_recv()
     loads[2].wait()
-    w_z = copy(wb.at[:, zc], wb.at[:, zc], zpair)
+    low, high = pl.ds(0, ny // 2), pl.ds(ny // 2, ny // 2)
+    w_z0 = copy(wb.at[low, zc], wb.at[low, zc], zdev(1))
+    w_z1 = copy(wb.at[high, zc], wb.at[high, zc], zdev(nz - 1))
     w_c1 = copy(wb.at[:, zc], wb.at[:, zc], core)
 
     counts_c.wait_recv()
@@ -189,6 +191,11 @@
         sums = sums + fyr[(y + ny - o - 1) % ny].astype(F32)
     plf[x] = (sums / jnp.maximum(column, 1.0)).astype(BF16)
     feat_x = [copy(plf.at[x], plf.at[x], xdev(o)) for o in range(1, nx)]
+
+    w_z0.wait_recv()
+    w_c2 = copy(wb.at[low, zc_far], wb.at[low, zc_far], core)
+    w_z1.wait_recv()
+    w_c3 = copy(wb.at[high, zc_far], wb.at[high, zc_far], core)
 
     sums = gys[y].astype(F32)
     for o, r in enumerate(cot_y):
@@ -211,10 +218,9 @@
         span = slice(n, n + step)
         wide = tk[:, :, span].reshape(rows, step).astype(F32) + dot(pooled, w_in[:, span])
         hid[:, span] = wide.astype(BF16)
-    w_z.wait_recv()
-    w_c2 = copy(wb.at[:, zc_far], wb.at[:, zc_far], core)
     w_c1.wait_recv()
     w_c2.wait_recv()
+    w_c3.wait_recv()
     queries = dot(hid[...], wb[...].reshape(d, cols)).astype(BF16)
     head_rows = pl.ds(pl.multiple_of(x * cols, cols), cols)
     tail_rows = pl.ds(pl.multiple_of(nx * cols + x * cols, cols), cols)
@@ -247,6 +253,8 @@
         up[k] = unp[k * TOK : (k + 1) * TOK]
     unp_x = [copy(up.at[(x + o) % nx], ur.at[x], xdev(o)) for o in range(1, nx)]
 
+    for n in range(0, d, 2 * TOK):
+        hidt[n : n + 2 * TOK] = hid[:, n : n + 2 * TOK].T
     for r in cot_x:
         r.wait_recv()
     pooled_grad = plg[...].reshape(rows, HEAD)
@@ -269,7 +277,7 @@
     for zk in range(2):
         for yk in range(ny):
             k = yk * 2 + zk
-            term = dot(hid[:, 2 * TOK * k : 2 * TOK * (k + 1)], q_grad, ((0,), (0,))).astype(BF16)
+            term = dot(hidt[2 * TOK * k : 2 * TOK * (k + 1)], q_grad).astype(BF16)
             for ck in range(2):
                 ga[ck, yk, zk] = term[TOK * ck : TOK * (ck + 1), :HEAD]
                 for q in range(nzh):
@@ -277,13 +285,6 @@
                     gb[ck, zk, q, yk] = term[at : at + quarter, HEAD:]
         grad_b.append(copy(gb.at[1 - c, zk], gcb.at[zk], core))
     grad_a = copy(ga.at[1 - c], gca, core)
-
-    sums = up[x].astype(F32)
-    for o, r in enumerate(unp_x):
-        r.wait_recv()
-        sums = sums + ur[(x + nx - o - 1) % nx].astype(F32)
-    ub[y, zc] = sums.astype(BF16)
-    unp_y = [copy(ub.at[y, zc], ub.at[y, zc], ydev(o)) for o in range(1, ny)]
 
     for zk in range(2):
         grad_b[zk].wait_recv()
@@ -295,10 +296,13 @@
         gsa[k] = (ga[c, k].astype(F32) + gca[k].astype(F32)).astype(BF16)
     ga_y = [copy(gsa.at[(y + o) % ny], gya.at[y], ydev(o)) for o in range(1, ny)]
 
-    for r in unp_y:
-        r.wait_recv()
-    unp_z = copy(ub.at[:, zc], ub.at[:, zc], zpair)
-    unp_c1 = copy(ub.at[:, zc], ub.at[:, zc], core)
+    sums = up[x].astype(F32)
+    for o, r in enumerate(unp_x):
+        r.wait_recv()
+        sums = sums + ur[(x + nx - o - 1) % nx].astype(F32)
+    ub[y, zc] = sums.astype(BF16)
+    unp_y = [copy(ub.at[y, zc], ub.at[y, zc], ydev(o)) for o in range(1, ny)]
+
 
     sums = gsb[z, zh].astype(F32)
     for o, r in enumerate(gb_z):
@@ -315,8 +319,10 @@
             ra[zk, q] = sums[zk, quarter * q : quarter * (q + 1)].astype(BF16)
     qa_z = [copy(ra.at[zslot(o)], qa.at[zz], zdev(o)) for o in range(1, nz)]
 
-    unp_z.wait_recv()
-    unp_c2 = copy(ub.at[:, zc_far], ub.at[:, zc_far], core)
+    for r in unp_y:
+        r.wait_recv()
+    unp_z = copy(ub.at[:, zc], ub.at[:, zc], zpair)
+    unp_c1 = copy(ub.at[:, zc], ub.at[:, zc], core)
 
     sums = rb[y].astype(F32)
     for o, r in enumerate(qb_y):
@@ -328,30 +334,27 @@
         r.wait_recv()
         sums = sums + qa[(zz + nz - o - 1) % nz].astype(F32)
     fx[x, zh, :, 0:HEAD] = sums.astype(BF16)
+    n_early = len(used)
     fin = [copy(fx.at[x, zh], fx.at[x, zh], xzdev(ox, oz)) for ox, oz in xz]
+
+    unp_z.wait_recv()
+    unp_c2 = copy(ub.at[:, zc_far], ub.at[:, zc_far], core)
 
     unp_c1.wait_recv()
     unp_c2.wait_recv()
-    stores = []
-    per = nb // 4
     for b in range(nb):
         owner = owners[b]
         member = (iota((TOK, BLOCK), 0) == clusters[b : b + 1, :]).astype(F32).astype(BF16)
         picked = dot(member, ub[owner // 4, owner % 4], ((0,), (0,)))
-        ob[b] = (fv[b].astype(F32) + picked).astype(BF16)
-        if b % per == per - 1:
-            span = pl.ds(b + 1 - per, per)
-            r = pltpu.make_async_copy(ob.at[span], p_out.at[span], here.at[6 + b // per])
-            r.start()
-            stores.append(r)
-
+        p_out[b] = (fv[b].astype(F32) + picked).astype(BF16)
+
+    for r in used[:n_early]:
+        r.wait_send()
     for r in fin:
         r.wait_recv()
     for k in range(nx):
         fin_out[:, cols * k : cols * (k + 1)] = fx[k].reshape(TOK, cols).astype(F32)
-    for r in stores:
-        r.wait()
-    for r in used:
+    for r in used[n_early:]:
         r.wait_send()
 
 
@@ -368,11 +371,11 @@
     side = (ny, TOK, HEAD)
     scratch = [
         v(nb, BLOCK, HEAD), v(nb, BLOCK, HEAD), v(*w_in.shape), v(*w_out.shape),
-        v(nb, BLOCK, HEAD), vf(ny, 8, HEAD),
+        vf(ny, 8, HEAD),
         v(*half), v(*half), v(*half), v(*half), vf(*half), vf(*half),
         v(*side), v(*side), v(*side), v(*side), v(*side), v(*side), v(*side), v(*side),
         vf(ny, 8, HEAD), vf(8, HEAD), vf(8, HEAD), vf(8, HEAD), vf(8, HEAD),
-        v(ny, 4, TOK, cols), v(nx, TOK, d), v(nx, TOK, HEAD), v(nx, TOK, HEAD), v(nx * TOK, d),
+        v(ny, 4, TOK, cols), v(nx, TOK, d), v(nx, TOK, HEAD), v(nx, TOK, HEAD), v(nx * TOK, d), v(d, nx * TOK),
         v(nx, TOK, HEAD), v(nx, TOK, HEAD), v(ny, 4, TOK, HEAD),
         v(2, ny, 2, TOK, HEAD), v(2, 2, nzh, ny, quarter, HEAD),
         v(ny, 2, TOK, HEAD), v(2, nzh, ny, quarter, HEAD),
@@ -381,7 +384,7 @@
         v(2, nzh, quarter, HEAD), v(ny, quarter, HEAD), v(nz, quarter, HEAD), v(ny, quarter, HEAD),
         v(nx, nzh, quarter, cols),
         pltpu.SemaphoreType.DMA((n_sem,)), pltpu.SemaphoreType.DMA((n_sem,)),
-        pltpu.SemaphoreType.DMA((10,)),
+        pltpu.SemaphoreType.DMA((6,)),
     ]
     vmem = pl.BlockSpec(memory_space=pltpu.VMEM)
     smem = pl.BlockSpec(memory_space=pltpu.SMEM)
@@ -389,11 +392,11 @@
     return pl.pallas_call(
         functools.partial(layer_kernel, nx, nzh, ny, n_sem),
         out_shape=(
-            jax.ShapeDtypeStruct((nb, BLOCK, HEAD), BF16),
-            jax.ShapeDtypeStruct((TOK, nx * cols), F32),
+            pltpu.VMEM((nb, BLOCK, HEAD), BF16),
+            pltpu.VMEM((TOK, nx * cols), F32),
         ),
         in_specs=[smem, smem, smem, vmem] + [hbm] * 6,
-        out_specs=(hbm, vmem),
+        out_specs=(vmem, vmem),
         scratch_shapes=scratch,
         compiler_params=pltpu.CompilerParams(collective_id=0, has_side_effects=True),
     )(owners, first, last, clusters, w, tok, w_in, w_out, feat, cot)

time: 73.6 us -> 68.2 us (0.927)
  Pallas kernels: 67.7 us -> 64.4 us
  local copies, waits for them, and re-layouts: 3.66 us -> 2.33 us
    pallas_call x1, Pallas kernels: 67.7 us -> 64.4 us  [layer(): pl.pallas_call(functools.partial(layer_kernel, nx, nzh, ny, n_sem), out_s...]
    unnamed x6 -> x4, local copies, waits for them, and re-layouts: 3.66 us -> 2.33 us
where the time goes in v3:
time: 68.2 us; the launch traced here: 68 us
  Pallas kernels  64.4 us (94%)
  local copies, waits for them, and re-layouts  2.33 us (3%)
    pallas_call x1, Pallas kernels, layer(): pl.pallas_call(functools.partial(layer_kernel, nx, nzh, ny, n_sem), out_s...  64.4 us
    unnamed x4, local copies, waits for them, and re-layouts  2.33 us

profile of v3, /device:TPU:1, one launch (start us, length us, event | category | flops | bytes accessed | tf_op | source)
XLA Modules:
  0.0 68.0 jit_solution(15965970612544156707)
XLA Ops:
  0.6 0.0 copy-start
  0.6 0.6 copy-done
  1.3 0.6 select_reduce_fusion
  1.9 64.4 %shard_map.95 = (bf16[32,128,128]{2,1,0:T(8,128)(2,1)S(1)}, f32[64,1024]{1,0:T(8,128)S(1)}) custom-call(s32[32]{0:T(128)} %owners.1, s32[32]{0:T(128)} %get-tuple-element.7.first, s32[32]{0:T(128)} %get-tuple-element.6.last, s32[32,128]{1,0:T(8,128)} %bitcast.7, bf16[64,1024]{1,0:T(8,128)(2,1)} %w.1, bf16[64,2048]{1,0:T(8,128)(2,1)} %tok.1, ...), custom_call_target="tpu_custom_call" | custom-call | tf_op jit(solution)/shard_map/pallas_call | solution.py:392
  66.3 1.0 %copy.12 = bf16[4096,128]{1,0:T(8,128)(2,1)} copy(bf16[4096,128]{1,0:T(8,128)(2,1)S(1)} %bitcast.4) | data formatting | bytes 2097152
  67.3 0.7 %copy.13 = f32[64,1024]{1,0:T(8,128)} copy(f32[64,1024]{1,0:T(8,128)S(1)} %get-tuple-element.9) | data formatting | bytes 524288
Async XLA Ops:
  0.6 0.7 copy-start

commit v4 on v3

--- a/solution.py
+++ b/solution.py
@@ -27,9 +27,9 @@
 
 def layer_kernel(
     nx, nzh, ny, n_sem,
-    owners, first, last, clusters, w, tok, w_in_hbm, w_out_hbm, feat_hbm, cot_hbm,
+    owners_hbm, clusters_hbm, w, tok, w_in_hbm, w_out_hbm, feat_hbm, cot_hbm,
     p_out, fin_out,
-    fv, cv, w_in, w_out, cnt,
+    owners, owner_row, ends, ends_s, clusters, fv, cv, w_in, w_out, cnt,
     pf, pg, pcf, pcg, fown, gown, fzs, fzr, gzs, gzr, fys, fyr, gys, gyr,
     cy, c1, cr, c2, cq, wb, tk, plf, plg, hid, hidt, up, ur, ub,
     ga, gb, gca, gcb, gsa, gsb, gya, gzb, ra, rb, qa, qb, fx,
@@ -49,7 +49,17 @@
     d = hid.shape[1]
     cols = 2 * HEAD
     quarter = TOK // nzh
-    nb = owners.shape[0]
+    nb = fv.shape[0]
+
+    loads = [
+        pltpu.make_async_copy(feat_hbm, fv, here.at[0]),
+        pltpu.make_async_copy(cot_hbm, cv, here.at[1]),
+        pltpu.make_async_copy(owners_hbm, owner_row, here.at[6]),
+        pltpu.make_async_copy(clusters_hbm, clusters, here.at[7]),
+        pltpu.make_async_copy(owners_hbm, owners, here.at[8]),
+    ]
+    for r in loads[2:] + loads[:2]:
+        r.start()
 
     core = (g, s + 1 - 2 * c)
     zpair = (g, s + 2 - 4 * z)
@@ -91,16 +101,24 @@
     for dev in peers:
         pl.semaphore_signal(barrier, inc=1, device_id=dev, device_id_type=MESH)
     mine = pl.ds(pl.multiple_of(x * cols, cols), cols)
-    loads = [
-        pltpu.make_async_copy(feat_hbm, fv, here.at[0]),
-        pltpu.make_async_copy(cot_hbm, cv, here.at[1]),
+    weights = [
         pltpu.make_async_copy(w.at[:, mine], wb.at[y, zc], here.at[2]),
         pltpu.make_async_copy(tok, tk.at[x], here.at[3]),
         pltpu.make_async_copy(w_in_hbm, w_in, here.at[4]),
         pltpu.make_async_copy(w_out_hbm, w_out, here.at[5]),
     ]
-    for r in loads:
+    for r in weights:
         r.start()
+    loads[2].wait()
+    at = iota((4 * ny, nb), 1)
+    named = jnp.broadcast_to(owner_row[...], (4 * ny, nb)) == iota((4 * ny, nb), 0)
+    at = at.astype(F32)
+    first = jnp.min(jnp.where(named, at, float(nb)), axis=1, keepdims=True)
+    last = jnp.max(jnp.where(named, at, -1.0), axis=1, keepdims=True)
+    ends[0] = jnp.broadcast_to(first.astype(jnp.int32), (4 * ny, HEAD))
+    ends[1] = jnp.broadcast_to(last.astype(jnp.int32), (4 * ny, HEAD))
+    to_scalar = pltpu.make_async_copy(ends, ends_s, here.at[9])
+    to_scalar.start()
     cnt[...] = jnp.zeros_like(cnt)
     pl.semaphore_wait(barrier, len(peers))
 
@@ -112,8 +130,9 @@
     def pooled_sum(yk, zk, ck):
         owner = yk * 4 + zk * 2 + ck
         member, feats, cots = [], [], []
-        b0, b1 = first[owner], last[owner]
-        for at, valid in ((jnp.minimum(b0, nb - 1), b0 < nb), (jnp.maximum(b1, 0), b1 > b0)):
+        b0, b1 = ends_s[0, owner, 0], ends_s[1, owner, 0]
+        for at, valid in ((b0, b0 < nb), (b1, b1 > b0)):
+            at = jnp.minimum(jnp.maximum(at, 0), nb - 1)
             labels = jnp.where(valid, clusters[pl.ds(at, 1), :], -1)
             member.append((iota((TOK, BLOCK), 0) == labels).astype(F32).astype(BF16))
             feats.append(fv[at])
@@ -125,8 +144,9 @@
         cnt[yk, pl.ds(zk * 2 + ck, 1), 0:TOK] = dot(ones, member, ((1,), (1,)))[:1]
         return dot(member, both)
 
-    loads[0].wait()
-    loads[1].wait()
+    to_scalar.wait()
+    for k in (3, 4, 0, 1):
+        loads[k].wait()
     for yk in range(ny):
         for zk in range(2):
             v = pooled_sum(yk, zk, 1 - c)
@@ -164,7 +184,7 @@
 
     for r in w_y:
         r.wait_recv()
-    loads[2].wait()
+    weights[0].wait()
     low, high = pl.ds(0, ny // 2), pl.ds(ny // 2, ny // 2)
     w_z0 = copy(wb.at[low, zc], wb.at[low, zc], zdev(1))
     w_z1 = copy(wb.at[high, zc], wb.at[high, zc], zdev(nz - 1))
@@ -204,7 +224,7 @@
     plg[x] = sums.astype(BF16)
     cot_x = [copy(plg.at[x], plg.at[x], xdev(o)) for o in range(1, nx)]
 
-    for r in loads[3:]:
+    for r in weights[1:]:
         r.wait()
     for r in tok_x:
         r.wait_recv()
@@ -343,7 +363,7 @@
     unp_c1.wait_recv()
     unp_c2.wait_recv()
     for b in range(nb):
-        owner = owners[b]
+        owner = owners[0, b]
         member = (iota((TOK, BLOCK), 0) == clusters[b : b + 1, :]).astype(F32).astype(BF16)
         picked = dot(member, ub[owner // 4, owner % 4], ((0,), (0,)))
         p_out[b] = (fv[b].astype(F32) + picked).astype(BF16)
@@ -358,18 +378,21 @@
         r.wait_send()
 
 
-def layer(owners, first, last, clusters, w, tok, w_in, w_out, feat, cot, nzh, ny):
+def layer(owners, clusters, w, tok, w_in, w_out, feat, cot, nzh, ny):
     nx, nz = NX, 2 * nzh
     d = w_in.shape[1]
     cols = 2 * HEAD
     quarter = TOK // nzh
-    nb = owners.shape[0]
+    nb = clusters.shape[0]
     n_sem = 20 + 9 * (ny - 1) + 4 * (nx - 1) + 2 * (nz - 1) + nx * nzh
     v = lambda *shape: pltpu.VMEM(shape, BF16)
     vf = lambda *shape: pltpu.VMEM(shape, F32)
     half = (2, ny, TOK, HEAD)
     side = (ny, TOK, HEAD)
     scratch = [
+        pltpu.SMEM((1, nb), jnp.int32), pltpu.VMEM((1, nb), jnp.int32),
+        pltpu.VMEM((2, 4 * ny, HEAD), jnp.int32), pltpu.SMEM((2, 4 * ny, HEAD), jnp.int32),
+        pltpu.VMEM(clusters.shape, jnp.int32),
         v(nb, BLOCK, HEAD), v(nb, BLOCK, HEAD), v(*w_in.shape), v(*w_out.shape),
         vf(ny, 8, HEAD),
         v(*half), v(*half), v(*half), v(*half), vf(*half), vf(*half),
@@ -384,10 +407,9 @@
         v(2, nzh, quarter, HEAD), v(ny, quarter, HEAD), v(nz, quarter, HEAD), v(ny, quarter, HEAD),
         v(nx, nzh, quarter, cols),
         pltpu.SemaphoreType.DMA((n_sem,)), pltpu.SemaphoreType.DMA((n_sem,)),
-        pltpu.SemaphoreType.DMA((6,)),
+        pltpu.SemaphoreType.DMA((10,)),
     ]
     vmem = pl.BlockSpec(memory_space=pltpu.VMEM)
-    smem = pl.BlockSpec(memory_space=pltpu.SMEM)
     hbm = pl.BlockSpec(memory_space=pl.ANY)
     return pl.pallas_call(
         functools.partial(layer_kernel, nx, nzh, ny, n_sem),
@@ -395,28 +417,46 @@
             pltpu.VMEM((nb, BLOCK, HEAD), BF16),
             pltpu.VMEM((TOK, nx * cols), F32),
         ),
-        in_specs=[smem, smem, smem, vmem] + [hbm] * 6,
+        in_specs=[hbm] * 8,
         out_specs=(vmem, vmem),
         scratch_shapes=scratch,
         compiler_params=pltpu.CompilerParams(collective_id=0, has_side_effects=True),
-    )(owners, first, last, clusters, w, tok, w_in, w_out, feat, cot)
+    )(owners, clusters, w, tok, w_in, w_out, feat, cot)
+
+
+def place_kernel(p_in, q_in, p_out, q_out, sems):
+    copies = [
+        pltpu.make_async_copy(p_in, p_out, sems.at[0]),
+        pltpu.make_async_copy(q_in, q_out, sems.at[1]),
+    ]
+    for r in copies:
+        r.start()
+    for r in copies:
+        r.wait()
+
+
+def place(p, q):
+    hbm = pl.BlockSpec(memory_space=pl.ANY)
+    return pl.pallas_call(
+        place_kernel,
+        out_shape=(jax.ShapeDtypeStruct(p.shape, p.dtype), jax.ShapeDtypeStruct(q.shape, q.dtype)),
+        in_specs=[pl.BlockSpec(memory_space=pltpu.VMEM)] * 2,
+        out_specs=(hbm, hbm),
+        scratch_shapes=[pltpu.SemaphoreType.DMA((2,))],
+    )(*(pltpu.with_memory_space_constraint(v, pltpu.VMEM) for v in (p, q)))
 
 
 def local(tokens, w_qk, w_in, w_out, particles, cotangent, clusters, owners):
     n_shard = lax.axis_size("shard")
     nzh = lax.axis_size("group") // NX
     nb = owners.shape[0]
-    ids = (n_shard, nb)
-    at = iota(ids, 1)
-    named = jnp.broadcast_to(owners[None, :], ids) == iota(ids, 0)
-    first = jnp.min(jnp.where(named, at, nb), axis=1)
-    last = jnp.max(jnp.where(named, at, -1), axis=1)
     feat = particles.reshape(nb, BLOCK, -1)
     cot = cotangent.reshape(nb, BLOCK, -1)
     out, qk_grad = layer(
-        owners, first, last, clusters.reshape(nb, BLOCK), w_qk, tokens, w_in, w_out, feat, cot,
+        owners.reshape(1, nb), clusters.reshape(nb, BLOCK), w_qk, tokens, w_in, w_out, feat, cot,
         nzh, n_shard // 4,
     )
+    out, qk_grad = place(out, qk_grad)
     return (out.reshape(particles.shape), qk_grad)
 
 

time: 68.2 us -> 65.7 us (0.963)
  local copies, waits for them, and re-layouts: 2.33 us -> 0 us
    unnamed x4 -> x0, local copies, waits for them, and re-layouts: 2.33 us -> none
    pallas_call x0 -> x1, Pallas kernels: none -> 1.07 us  [place(): pl.pallas_call(place_kernel, out_shape=(jax.ShapeDtypeStruct(p.shape, p.d...]
where the time goes in v4:
time: 65.7 us; the launch traced here: 65.6 us
  Pallas kernels  64.9 us (99%)
    pallas_call x1, Pallas kernels, layer(): pl.pallas_call(functools.partial(layer_kernel, nx, nzh, ny, n_sem), out_s...  63.9 us

profile of v4, /device:TPU:1, one launch (start us, length us, event | category | flops | bytes accessed | tf_op | source)
XLA Modules:
  0.0 65.6 jit_solution(11280057420294502993)
XLA Ops:
  0.6 63.9 %shard_map.95 = (bf16[32,128,128]{2,1,0:T(8,128)(2,1)S(1)}, f32[64,1024]{1,0:T(8,128)S(1)}) custom-call(s32[1,32]{1,0:T(1,128)} %bitcast.8, s32[32,128]{1,0:T(8,128)} %bitcast.7, bf16[64,1024]{1,0:T(8,128)(2,1)} %w.1, bf16[64,2048]{1,0:T(8,128)(2,1)} %tok.1, bf16[128,2048]{1,0:T(8,128)(2,1)} %w_in_hbm.1, bf16[2048,128]{1,0:T(8,128)(2,1)} %w_out_hbm.1, ...), custom_call_target="tpu_custom_call" | custom-call | tf_op jit(solution)/shard_map/pallas_call | solution.py:414
  64.5 1.1 %shard_map.96 = (bf16[32,128,128]{2,1,0:T(8,128)(2,1)}, f32[64,1024]{1,0:T(8,128)}) custom-call(bf16[32,128,128]{2,1,0:T(8,128)(2,1)S(1)} %get-tuple-element.6.p_in, f32[64,1024]{1,0:T(8,128)S(1)} %get-tuple-element.7.q_in), custom_call_target="tpu_custom_call" | custom-call | tf_op jit(solution)/shard_map/pallas_call | solution.py:440

commit v5 on v4

--- a/solution.py
+++ b/solution.py
@@ -23,6 +23,10 @@
 
 def iota(shape, dim):
     return lax.broadcasted_iota(jnp.int32, shape, dim)
+
+
+def far(n):
+    return sorted(range(1, n), key=lambda o: -min(o, n - o))
 
 
 def layer_kernel(
@@ -82,6 +86,7 @@
         return (((x + ox) % nx) * nzh + (zh + oz) % nzh, s)
 
     xz = [(ox, oz) for ox in range(nx) for oz in range(nzh) if ox or oz]
+    xz.sort(key=lambda o: -min(o[0], nx - o[0]) - 2 * min(o[1], nzh - o[1]))
     used = []
 
     def copy(src, dst, dev):
@@ -122,8 +127,8 @@
     cnt[...] = jnp.zeros_like(cnt)
     pl.semaphore_wait(barrier, len(peers))
 
-    w_y = [copy(w.at[:, mine], wb.at[y, zc], ydev(o)) for o in range(1, ny)]
-    tok_x = [copy(tok, tk.at[x], xdev(o)) for o in range(1, nx)]
+    w_y = [copy(w.at[:, mine], wb.at[y, zc], ydev(o)) for o in far(ny)]
+    tok_x = [copy(tok, tk.at[x], xdev(o)) for o in far(nx)]
 
     ones = jnp.ones((8, 2 * BLOCK), BF16)
 
@@ -147,38 +152,46 @@
     to_scalar.wait()
     for k in (3, 4, 0, 1):
         loads[k].wait()
-    for yk in range(ny):
-        for zk in range(2):
+    pool_f = {}
+    for zk in (1 - z, z):
+        for yk in range(ny):
             v = pooled_sum(yk, zk, 1 - c)
             pf[zk, yk] = v[:, :HEAD].astype(BF16)
             pg[zk, yk] = v[:, HEAD:].astype(BF16)
-    pool_f = copy(pf, pcf, core)
+        pool_f[len(pool_f)] = copy(pf.at[zk], pcf.at[zk], core)
     pool_g = copy(pg, pcg, core)
-    for yk in range(ny):
-        for zk in range(2):
+    feat_z = []
+    for zk in (1 - z, z):
+        for yk in range(ny):
             v = pooled_sum(yk, zk, c)
             fown[zk, yk] = v[:, :HEAD]
             gown[zk, yk] = v[:, HEAD:]
-    counts_y = [copy(cnt.at[(y + o) % ny], cy.at[y], ydev(o)) for o in range(1, ny)]
-
-    pool_f.wait_recv()
-    for k in range(ny):
-        fzs[k] = (fown[1 - z, k] + pcf[1 - z, k].astype(F32)).astype(BF16)
-    feat_z = copy(fzs, fzr, zpair)
+        if not feat_z:
+            pool_f[0].wait_recv()
+            for o in far(ny) + [0]:
+                k = (y + o) % ny
+                fzs[k] = (fown[zk, k] + pcf[zk, k].astype(F32)).astype(BF16)
+                feat_z.append(copy(fzs.at[k], fzr.at[k], zpair))
+    counts_y = [copy(cnt.at[(y + o) % ny], cy.at[y], ydev(o)) for o in far(ny)]
+
     pool_g.wait_recv()
     for k in range(ny):
         gzs[k] = (gown[1 - z, k] + pcg[1 - z, k].astype(F32)).astype(BF16)
     cot_z = copy(gzs, gzr, zpair)
 
-    feat_z.wait_recv()
-    for k in range(ny):
+    pool_f[1].wait_recv()
+    feat_y = []
+    for o, r in zip(far(ny) + [0], feat_z):
+        k = (y + o) % ny
+        r.wait_recv()
         fys[k] = (fown[z, k] + pcf[z, k].astype(F32) + fzr[k].astype(F32)).astype(BF16)
-    feat_y = [copy(fys.at[(y + o) % ny], fyr.at[y], ydev(o)) for o in range(1, ny)]
+        if o:
+            feat_y.append(copy(fys.at[k], fyr.at[y], ydev(o)))
 
     total = cnt[y]
-    for o, r in enumerate(counts_y):
-        r.wait_recv()
-        total = total + cy[(y + ny - o - 1) % ny]
+    for o, r in zip(far(ny), counts_y):
+        r.wait_recv()
+        total = total + cy[(y + ny - o) % ny]
     c1[...] = total
     counts_c = copy(c1, cr, core)
 
@@ -197,7 +210,7 @@
     cot_z.wait_recv()
     for k in range(ny):
         gys[k] = (gown[z, k] + pcg[z, k].astype(F32) + gzr[k].astype(F32)).astype(BF16)
-    cot_y = [copy(gys.at[(y + o) % ny], gyr.at[y], ydev(o)) for o in range(1, ny)]
+    cot_y = [copy(gys.at[(y + o) % ny], gyr.at[y], ydev(o)) for o in far(ny)]
 
     counts_z.wait_recv()
     count = c2[...] + cq[...]
@@ -206,11 +219,11 @@
     column = jnp.sum(jnp.where(eye, jnp.broadcast_to(row, (TOK, HEAD)), 0.0), axis=1, keepdims=True)
 
     sums = fys[y].astype(F32)
-    for o, r in enumerate(feat_y):
-        r.wait_recv()
-        sums = sums + fyr[(y + ny - o - 1) % ny].astype(F32)
+    for o, r in zip(far(ny), feat_y):
+        r.wait_recv()
+        sums = sums + fyr[(y + ny - o) % ny].astype(F32)
     plf[x] = (sums / jnp.maximum(column, 1.0)).astype(BF16)
-    feat_x = [copy(plf.at[x], plf.at[x], xdev(o)) for o in range(1, nx)]
+    feat_x = [copy(plf.at[x], plf.at[x], xdev(o)) for o in far(nx)]
 
     w_z0.wait_recv()
     w_c2 = copy(wb.at[low, zc_far], wb.at[low, zc_far], core)
@@ -218,11 +231,11 @@
     w_c3 = copy(wb.at[high, zc_far], wb.at[high, zc_far], core)
 
     sums = gys[y].astype(F32)
-    for o, r in enumerate(cot_y):
-        r.wait_recv()
-        sums = sums + gyr[(y + ny - o - 1) % ny].astype(F32)
+    for o, r in zip(far(ny), cot_y):
+        r.wait_recv()
+        sums = sums + gyr[(y + ny - o) % ny].astype(F32)
     plg[x] = sums.astype(BF16)
-    cot_x = [copy(plg.at[x], plg.at[x], xdev(o)) for o in range(1, nx)]
+    cot_x = [copy(plg.at[x], plg.at[x], xdev(o)) for o in far(nx)]
 
     for r in weights[1:]:
         r.wait()
@@ -271,7 +284,7 @@
     unp = unp.astype(BF16)
     for k in range(nx):
         up[k] = unp[k * TOK : (k + 1) * TOK]
-    unp_x = [copy(up.at[(x + o) % nx], ur.at[x], xdev(o)) for o in range(1, nx)]
+    unp_x = [copy(up.at[(x + o) % nx], ur.at[x], xdev(o)) for o in far(nx)]
 
     for n in range(0, d, 2 * TOK):
         hidt[n : n + 2 * TOK] = hid[:, n : n + 2 * TOK].T
@@ -310,34 +323,34 @@
         grad_b[zk].wait_recv()
         for q in range(nzh):
             gsb[zk, q] = (gb[c, zk, q].astype(F32) + gcb[zk, q].astype(F32)).astype(BF16)
-    gb_z = [copy(gsb.at[zslot(o)], gzb.at[zz], zdev(o)) for o in range(1, nz)]
+    gb_z = [copy(gsb.at[zslot(o)], gzb.at[zz], zdev(o)) for o in far(nz)]
     grad_a.wait_recv()
     for k in range(ny):
         gsa[k] = (ga[c, k].astype(F32) + gca[k].astype(F32)).astype(BF16)
-    ga_y = [copy(gsa.at[(y + o) % ny], gya.at[y], ydev(o)) for o in range(1, ny)]
+    ga_y = [copy(gsa.at[(y + o) % ny], gya.at[y], ydev(o)) for o in far(ny)]
 
     sums = up[x].astype(F32)
-    for o, r in enumerate(unp_x):
-        r.wait_recv()
-        sums = sums + ur[(x + nx - o - 1) % nx].astype(F32)
+    for o, r in zip(far(nx), unp_x):
+        r.wait_recv()
+        sums = sums + ur[(x + nx - o) % nx].astype(F32)
     ub[y, zc] = sums.astype(BF16)
-    unp_y = [copy(ub.at[y, zc], ub.at[y, zc], ydev(o)) for o in range(1, ny)]
+    unp_y = [copy(ub.at[y, zc], ub.at[y, zc], ydev(o)) for o in far(ny)]
 
 
     sums = gsb[z, zh].astype(F32)
-    for o, r in enumerate(gb_z):
-        r.wait_recv()
-        sums = sums + gzb[(zz + nz - o - 1) % nz].astype(F32)
+    for o, r in zip(far(nz), gb_z):
+        r.wait_recv()
+        sums = sums + gzb[(zz + nz - o) % nz].astype(F32)
     rb[...] = sums.astype(BF16)
-    qb_y = [copy(rb.at[(y + o) % ny], qb.at[y], ydev(o)) for o in range(1, ny)]
+    qb_y = [copy(rb.at[(y + o) % ny], qb.at[y], ydev(o)) for o in far(ny)]
     sums = gsa[y].astype(F32)
-    for o, r in enumerate(ga_y):
-        r.wait_recv()
-        sums = sums + gya[(y + ny - o - 1) % ny].astype(F32)
+    for o, r in zip(far(ny), ga_y):
+        r.wait_recv()
+        sums = sums + gya[(y + ny - o) % ny].astype(F32)
     for zk in range(2):
         for q in range(nzh):
             ra[zk, q] = sums[zk, quarter * q : quarter * (q + 1)].astype(BF16)
-    qa_z = [copy(ra.at[zslot(o)], qa.at[zz], zdev(o)) for o in range(1, nz)]
+    qa_z = [copy(ra.at[zslot(o)], qa.at[zz], zdev(o)) for o in far(nz)]
 
     for r in unp_y:
         r.wait_recv()
@@ -345,14 +358,14 @@
     unp_c1 = copy(ub.at[:, zc], ub.at[:, zc], core)
 
     sums = rb[y].astype(F32)
-    for o, r in enumerate(qb_y):
-        r.wait_recv()
-        sums = sums + qb[(y + ny - o - 1) % ny].astype(F32)
+    for o, r in zip(far(ny), qb_y):
+        r.wait_recv()
+        sums = sums + qb[(y + ny - o) % ny].astype(F32)
     fx[x, zh, :, HEAD : 2 * HEAD] = sums.astype(BF16)
     sums = ra[z, zh].astype(F32)
-    for o, r in enumerate(qa_z):
-        r.wait_recv()
-        sums = sums + qa[(zz + nz - o - 1) % nz].astype(F32)
+    for o, r in zip(far(nz), qa_z):
+        r.wait_recv()
+        sums = sums + qa[(zz + nz - o) % nz].astype(F32)
     fx[x, zh, :, 0:HEAD] = sums.astype(BF16)
     n_early = len(used)
     fin = [copy(fx.at[x, zh], fx.at[x, zh], xzdev(ox, oz)) for ox, oz in xz]
@@ -384,7 +397,7 @@
     cols = 2 * HEAD
     quarter = TOK // nzh
     nb = clusters.shape[0]
-    n_sem = 20 + 9 * (ny - 1) + 4 * (nx - 1) + 2 * (nz - 1) + nx * nzh
+    n_sem = 24 + 10 * (ny - 1) + 4 * (nx - 1) + 2 * (nz - 1) + nx * nzh
     v = lambda *shape: pltpu.VMEM(shape, BF16)
     vf = lambda *shape: pltpu.VMEM(shape, F32)
     half = (2, ny, TOK, HEAD)

time: 65.7 us -> 63.6 us (0.968)
  Pallas kernels: 64.9 us -> 62.8 us
    pallas_call x1, Pallas kernels: 63.9 us -> 61.8 us  [layer(): pl.pallas_call(functools.partial(layer_kernel, nx, nzh, ny, n_sem), out_s...]
where the time goes in v5:
time: 63.6 us; the launch traced here: 63.5 us
  Pallas kernels  62.8 us (99%)
  between operations  0.64 us (1%)
    pallas_call x1, Pallas kernels, layer(): pl.pallas_call(functools.partial(layer_kernel, nx, nzh, ny, n_sem), out_s...  61.8 us

profile of v5, /device:TPU:1, one launch (start us, length us, event | category | flops | bytes accessed | tf_op | source)
XLA Modules:
  0.0 63.5 jit_solution(9527898526480312564)
XLA Ops:
  0.6 61.8 %shard_map.95 = (bf16[32,128,128]{2,1,0:T(8,128)(2,1)S(1)}, f32[64,1024]{1,0:T(8,128)S(1)}) custom-call(s32[1,32]{1,0:T(1,128)} %bitcast.8, s32[32,128]{1,0:T(8,128)} %bitcast.7, bf16[64,1024]{1,0:T(8,128)(2,1)} %w.1, bf16[64,2048]{1,0:T(8,128)(2,1)} %tok.1, bf16[128,2048]{1,0:T(8,128)(2,1)} %w_in_hbm.1, bf16[2048,128]{1,0:T(8,128)(2,1)} %w_out_hbm.1, ...), custom_call_target="tpu_custom_call" | custom-call | tf_op jit(solution)/shard_map/pallas_call | solution.py:427
  62.4 1.1 %shard_map.96 = (bf16[32,128,128]{2,1,0:T(8,128)(2,1)}, f32[64,1024]{1,0:T(8,128)}) custom-call(bf16[32,128,128]{2,1,0:T(8,128)(2,1)S(1)} %get-tuple-element.6.p_in, f32[64,1024]{1,0:T(8,128)S(1)} %get-tuple-element.7.q_in), custom_call_target="tpu_custom_call" | custom-call | tf_op jit(solution)/shard_map/pallas_call | solution.py:453

commit v6 on v5

--- a/solution.py
+++ b/solution.py
@@ -175,9 +175,11 @@
     counts_y = [copy(cnt.at[(y + o) % ny], cy.at[y], ydev(o)) for o in far(ny)]
 
     pool_g.wait_recv()
-    for k in range(ny):
+    cot_z = []
+    for o in far(ny) + [0]:
+        k = (y + o) % ny
         gzs[k] = (gown[1 - z, k] + pcg[1 - z, k].astype(F32)).astype(BF16)
-    cot_z = copy(gzs, gzr, zpair)
+        cot_z.append(copy(gzs.at[k], gzr.at[k], zpair))
 
     pool_f[1].wait_recv()
     feat_y = []
@@ -207,10 +209,13 @@
     c2[...] = c1[...] + cr[...]
     counts_z = copy(c2, cq, zpair)
 
-    cot_z.wait_recv()
-    for k in range(ny):
+    cot_y = []
+    for o, r in zip(far(ny) + [0], cot_z):
+        k = (y + o) % ny
+        r.wait_recv()
         gys[k] = (gown[z, k] + pcg[z, k].astype(F32) + gzr[k].astype(F32)).astype(BF16)
-    cot_y = [copy(gys.at[(y + o) % ny], gyr.at[y], ydev(o)) for o in far(ny)]
+        if o:
+            cot_y.append(copy(gys.at[k], gyr.at[y], ydev(o)))
 
     counts_z.wait_recv()
     count = c2[...] + cq[...]
@@ -306,7 +311,7 @@
         q_parts.append(jnp.concatenate(q_row, axis=1))
     q_grad = jnp.concatenate(q_parts, axis=0)
 
-    grad_b = []
+    grad_a, grad_b = [], []
     for zk in range(2):
         for yk in range(ny):
             k = yk * 2 + zk
@@ -317,17 +322,21 @@
                     at = TOK * ck + quarter * q
                     gb[ck, zk, q, yk] = term[at : at + quarter, HEAD:]
         grad_b.append(copy(gb.at[1 - c, zk], gcb.at[zk], core))
-    grad_a = copy(ga.at[1 - c], gca, core)
+        grad_a.append(copy(ga.at[1 - c, :, zk], gca.at[:, zk], core))
 
     for zk in range(2):
         grad_b[zk].wait_recv()
         for q in range(nzh):
             gsb[zk, q] = (gb[c, zk, q].astype(F32) + gcb[zk, q].astype(F32)).astype(BF16)
     gb_z = [copy(gsb.at[zslot(o)], gzb.at[zz], zdev(o)) for o in far(nz)]
-    grad_a.wait_recv()
-    for k in range(ny):
+    for r in grad_a:
+        r.wait_recv()
+    ga_y = []
+    for o in far(ny) + [0]:
+        k = (y + o) % ny
         gsa[k] = (ga[c, k].astype(F32) + gca[k].astype(F32)).astype(BF16)
-    ga_y = [copy(gsa.at[(y + o) % ny], gya.at[y], ydev(o)) for o in far(ny)]
+        if o:
+            ga_y.append(copy(gsa.at[k], gya.at[y], ydev(o)))
 
     sums = up[x].astype(F32)
     for o, r in zip(far(nx), unp_x):
@@ -397,7 +406,7 @@
     cols = 2 * HEAD
     quarter = TOK // nzh
     nb = clusters.shape[0]
-    n_sem = 24 + 10 * (ny - 1) + 4 * (nx - 1) + 2 * (nz - 1) + nx * nzh
+    n_sem = 26 + 11 * (ny - 1) + 4 * (nx - 1) + 2 * (nz - 1) + nx * nzh
     v = lambda *shape: pltpu.VMEM(shape, BF16)
     vf = lambda *shape: pltpu.VMEM(shape, F32)
     half = (2, ny, TOK, HEAD)

time: 63.6 us -> 63.5 us (level)
  no operation moved by 1% of the time
where the time goes in v6:
time: 63.5 us; the launch traced here: 63.3 us
  Pallas kernels  62.7 us (99%)
  between operations  0.64 us (1%)
    pallas_call x1, Pallas kernels, layer(): pl.pallas_call(functools.partial(layer_kernel, nx, nzh, ny, n_sem), out_s...  61.6 us

profile of v6, /device:TPU:1, one launch (start us, length us, event | category | flops | bytes accessed | tf_op | source)
XLA Modules:
  0.0 63.3 jit_solution(138695089721192471)
XLA Ops:
  0.6 61.6 %shard_map.95 = (bf16[32,128,128]{2,1,0:T(8,128)(2,1)S(1)}, f32[64,1024]{1,0:T(8,128)S(1)}) custom-call(s32[1,32]{1,0:T(1,128)} %bitcast.8, s32[32,128]{1,0:T(8,128)} %bitcast.7, bf16[64,1024]{1,0:T(8,128)(2,1)} %w.1, bf16[64,2048]{1,0:T(8,128)(2,1)} %tok.1, bf16[128,2048]{1,0:T(8,128)(2,1)} %w_in_hbm.1, bf16[2048,128]{1,0:T(8,128)(2,1)} %w_out_hbm.1, ...), custom_call_target="tpu_custom_call" | custom-call | tf_op jit(solution)/shard_map/pallas_call | solution.py:436
  62.3 1.1 %shard_map.96 = (bf16[32,128,128]{2,1,0:T(8,128)(2,1)}, f32[64,1024]{1,0:T(8,128)}) custom-call(bf16[32,128,128]{2,1,0:T(8,128)(2,1)S(1)} %get-tuple-element.6.p_in, f32[64,1024]{1,0:T(8,128)S(1)} %get-tuple-element.7.q_in), custom_call_target="tpu_custom_call" | custom-call | tf_op jit(solution)/shard_map/pallas_call | solution.py:462
